TPU v7x, 256 devices: a whole 4x4x8 slice. The times are simulated.
256 devices in a mesh: tm: 8 (over z), paths: 32 (over y, x, core).
Axes of the slice: x: 4, y: 4, z: 8, core: 2. Of those that a mesh axis runs over, the one named last changes fastest.
Arguments:
- start_curve: float32 [80], replicated, may hold values from 0.02 to 0.06
- loadings: float32 [4, 80], replicated, may hold values from 0.2 to 1
- vols: float32 [40, 80], P('tm'), may hold values from 0.08 to 0.4
- shocks: float32 [40, 4, 65536], P('tm', None, 'paths'), may hold values from -5 to 5
- exercise_bits: int32 [40, 65536], P('tm', 'paths'), may hold values 0 or 1
- regress: float32 [40, 6], P('tm'), may hold values from -0.03 to 0.03
- date_slot: int32 [40], P('tm'), may hold values from 0 to 39, each once
- ck_rates: float32 [8, 80, 65536], P('tm', None, 'paths'), may hold values from 0.02 to 0.07
- ck_numer: float32 [8, 65536], P('tm', 'paths'), may hold values from 1 to 3
- ck_survive: float32 [8, 65536], P('tm', 'paths'), may hold values from 0.2 to 1
Outputs:
- vega: float32 [40, 80], P('tm')
- path_value: float32 [65536], P('paths')
Inputs may be any that keep to these rules, and one draw needn't show every extreme that they name: `date_slot`: each row of regress is named once: a permutation of the 40 rows.
All inputs are finite; a program needn't handle non-finite values. No bound on the sum of `exercise_bits` on one device may be relied on, other than what follows from the above.
Results may differ from a plain program's by a relative error of at most 0.0003.
Values sent between devices are 32-bit elements; how exact they have to be, the bound alone decides.
A program may use at most 128 MiB of HBM per device.

v0:
```python
import jax
import jax.numpy as jnp
from jax import lax
from jax.sharding import PartitionSpec as P

BLOCK = 256


ACCRUAL = 0.25
STRIKE = 0.04
SMOOTHING = 0.01
NOTIONAL = 100.0
HIGHEST = lax.Precision.HIGHEST


def copy_for_each(shard, axis):
    copies = jnp.broadcast_to(shard, (lax.axis_size(axis), *shard.shape))
    return lax.all_to_all(copies, axis, split_axis=0, concat_axis=0, tiled=True)


def of_everyone(shard, axis):
    everything = copy_for_each(shard, axis)
    return jnp.sum(everything, axis=0)


def joined_along(blocks, dim):
    lengths = list(blocks.shape[1:])
    lengths[dim] *= blocks.shape[0]
    return jnp.moveaxis(blocks, 0, dim).reshape(lengths)


def collect(shard, axis, dim):
    blocks = copy_for_each(shard, axis)
    return joined_along(blocks, dim)


def passed_along(value, axis, steps):
    count = lax.axis_size(axis)
    initial, last = (max(0, -steps), min(count, count - steps))
    return lax.ppermute(value, axis, [(source, source + steps) for source in range(initial, last)])


def segment(
    rates_in,
    numeraire,
    survival,
    vol_rows,
    shock_rows,
    flag_rows,
    weight_rows,
    loadings,
    first_date,
):
    forwards = rates_in.shape[0]
    positions = jnp.arange(forwards, dtype=jnp.int32)
    triangle = (positions[:, None] >= positions[None, :]).astype(jnp.float32)
    factor_loads = loadings / jnp.sqrt(jnp.sum(loadings * loadings, axis=0, keepdims=True))
    current = rates_in
    path_total = jnp.zeros(numeraire.shape, jnp.float32)
    for offset_date in range(vol_rows.shape[0]):
        date_index = first_date + offset_date
        opening = 2 * date_index + 1
        earlier = jnp.where(date_index == 0, 0, 2 * date_index - 1)
        horizon = jnp.where(date_index == 0, ACCRUAL, 2.0 * ACCRUAL)
        growth = jnp.log1p(ACCRUAL * current)
        fixing = ((positions >= earlier) & (positions < opening)).astype(jnp.float32)
        numeraire = numeraire * jnp.exp(jnp.sum(fixing[:, None] * growth, axis=0))
        living = (positions >= opening).astype(jnp.float32)
        sigma = vol_rows[offset_date] * living
        scaled = ACCRUAL * current * sigma[:, None] / (1.0 + ACCRUAL * current)
        running = jnp.einsum(
            "ij,fjp->fip", triangle, factor_loads[:, :, None] * scaled[None], precision=HIGHEST
        )
        drift = sigma[:, None] * jnp.sum(factor_loads[:, :, None] * running, axis=0)
        noise = jnp.einsum("fi,fp->ip", factor_loads, shock_rows[offset_date], precision=HIGHEST)
        exponent = (
            horizon * drift
            - 0.5 * horizon * (sigma * sigma)[:, None]
            + jnp.sqrt(horizon) * sigma[:, None] * noise
        )
        current = current * jnp.exp(exponent)
        discount = jnp.dot(
            triangle, living[:, None] * jnp.log1p(ACCRUAL * current), precision=HIGHEST
        )
        bonds = jnp.exp(-discount)
        annuity = ACCRUAL * jnp.sum(living[:, None] * bonds, axis=0)
        floating = 1.0 - bonds[forwards - 1]
        exercise = floating - STRIKE * annuity
        moneyness = (floating / annuity - STRIKE) / SMOOTHING
        basis = jnp.stack(
            [
                jnp.ones_like(moneyness),
                moneyness,
                moneyness * moneyness,
                annuity,
                annuity * moneyness,
                annuity * moneyness * moneyness,
            ]
        )
        continuation = jnp.einsum("b,bp->p", weight_rows[offset_date], basis, precision=HIGHEST)
        chance = flag_rows[offset_date] * jax.nn.sigmoid((exercise - continuation) / SMOOTHING)
        path_total = path_total + NOTIONAL * survival * chance * exercise / numeraire
        survival = survival * (1.0 - chance)
    return (current, numeraire, survival, path_total)


def pullback(
    opening_state,
    vol_rows,
    shock_rows,
    flag_rows,
    weight_rows,
    loadings,
    first_date,
    adjoint_in,
    path_weight,
):

    def runner(rates_in, numer_in, survive_in, local_vols):
        return segment(
            rates_in,
            numer_in,
            survive_in,
            local_vols,
            shock_rows,
            flag_rows,
            weight_rows,
            loadings,
            first_date,
        )

    outputs, reverse_map = jax.vjp(
        runner, opening_state[0], opening_state[1], opening_state[2], vol_rows
    )
    gradient = reverse_map(
        (adjoint_in[0], adjoint_in[1], adjoint_in[2], jnp.full_like(outputs[3], path_weight))
    )
    return ((gradient[0], gradient[1], gradient[2]), gradient[3], outputs[3])


def add_values(partial_values):
    return of_everyone(partial_values, "tm")


def local(
    start_curve,
    loadings,
    vols,
    shocks,
    exercise_bits,
    regress,
    date_slot,
    ck_rates,
    ck_numer,
    ck_survive,
):
    shard_count = lax.axis_size("tm")
    group_count = lax.axis_size("paths")
    device_index = lax.axis_index("tm")
    per_shard = vols.shape[0]
    path_count = shocks.shape[2]
    forwards = vols.shape[1]
    date_count = per_shard * shard_count
    path_weight = NOTIONAL / (path_count * group_count)
    table = collect(regress, "tm", 0)
    onehot = (date_slot[:, None] == jnp.arange(date_count, dtype=jnp.int32)[None, :]).astype(
        jnp.float32
    )
    weight_rows = jnp.dot(onehot, table, precision=HIGHEST)
    flag_rows = exercise_bits.astype(jnp.float32)
    received = passed_along((ck_rates[0], ck_numer[0], ck_survive[0]), "tm", 1)
    is_first = device_index == 0
    opening_state = (
        jnp.where(is_first, start_curve[:, None], received[0]),
        jnp.where(is_first, 1.0, received[1]),
        jnp.where(is_first, 1.0, received[2]),
    )
    first_date = device_index * per_shard
    block_count = path_count // BLOCK
    section_count = block_count + shard_count - 1
    zero_adjoint = (
        jnp.zeros((forwards, BLOCK), jnp.float32),
        jnp.zeros((BLOCK,), jnp.float32),
        jnp.zeros((BLOCK,), jnp.float32),
    )

    def run_section(section_index, loop_state):
        incoming, vega_total, chain_values = loop_state
        block_index = section_index - (shard_count - 1 - device_index)
        in_range = (block_index >= 0) & (block_index < block_count)
        offset = jnp.clip(block_index, 0, block_count - 1) * BLOCK

        def slice_block(array_in, axis_number):
            return lax.dynamic_slice_in_dim(array_in, offset, BLOCK, axis_number)

        def masked(array_in):
            return jnp.where(in_range, array_in, 0.0)

        block_state = (
            slice_block(opening_state[0], 1),
            slice_block(opening_state[1], 0),
            slice_block(opening_state[2], 0),
        )
        outgoing, block_vega, block_value = pullback(
            block_state,
            vols,
            slice_block(shocks, 2),
            slice_block(flag_rows, 1),
            weight_rows,
            loadings,
            first_date,
            incoming,
            path_weight,
        )
        passed = passed_along(jax.tree.map(masked, outgoing), "tm", -1)
        previous = slice_block(chain_values, 0)
        chain_values = lax.dynamic_update_slice_in_dim(
            chain_values, jnp.where(in_range, block_value, previous), offset, 0
        )
        return (passed, vega_total + masked(block_vega), chain_values)

    initial_state = (zero_adjoint, jnp.zeros_like(vols), jnp.zeros((path_count,), jnp.float32))
    final_state = lax.fori_loop(0, section_count, run_section, initial_state)
    vega_part = final_state[1]
    chain_values = final_state[2]
    path_value = add_values(chain_values)
    vega = of_everyone(vega_part, "paths")
    return (vega, path_value)


def solution(mesh):
    return jax.shard_map(
        local,
        mesh=mesh,
        in_specs=(
            P(),
            P(),
            P("tm", None),
            P("tm", None, "paths"),
            P("tm", "paths"),
            P("tm", None),
            P("tm"),
            P("tm", None, "paths"),
            P("tm", "paths"),
            P("tm", "paths"),
        ),
        out_specs=(P("tm", None), P("paths")),
        check_vma=False,
    )
```

profile of v0, /device:TPU:1, one launch (start us, length us, event | category | flops | bytes accessed | tf_op | source)
XLA Modules:
  0.0 460.5 jit_solution(14782624434557097175)
XLA Ops:
  0.6 4.4 collective-permute-start.3
  5.0 3.6 collective-permute-start.4
  10.0 6.5 %all-to-all-start = ((f32[8,5,6]{1,2,0:T(8,128)}), f32[8,5,6]{1,2,0:T(8,128)S(1)}, u32[]{:S(2)}, u32[]{:S(2)}) async-start(f32[8,5,6]{1,2,0:T(8,128)} %broadcast_in_dim.457), calls=%async_computation | async-start | bytes 65536 | tf_op jit(solution)/shard_map/all_to_all | solution.py:18
  16.5 3.4 collective-permute-start.5
  20.8 6.9 %all-to-all-done = f32[8,5,6]{1,2,0:T(8,128)S(1)} async-done(((f32[8,5,6]{1,2,0:T(8,128)}), f32[8,5,6]{1,2,0:T(8,128)S(1)}, u32[]{:S(2)}, u32[]{:S(2)}) %all-to-all-start) | async-done | bytes 992 | tf_op jit(solution)/shard_map/all_to_all | solution.py:18
  30.1 376.7 %while.25 = (s32[]{:T(128)}, f32[80,256]{1,0:T(8,128)S(1)}, f32[256]{0:T(256)S(1)}, f32[256]{0:T(256)S(1)}, f32[5,80]{1,0:T(8,128)S(1)}, /*index=5*/f32[2048]{0:...) while((s32[]{:T(128)}, f32[80,256]{1,0:T(8,128)S(1)}, ...), condition=%wide.region_42.43_spmd.clone, body=%wide.region_1.42_spmd.clone.sunk | while | flops 996735552 | bytes 12365991 | solution.py:223
  47.5 1.3 collective-permute-start.1
  48.8 1.3 collective-permute-start.2
  50.7 3.7 collective-permute-done.2
  71.7 1.3 collective-permute-start.1
  73.0 1.3 collective-permute-start.2
  74.9 4.0 collective-permute-done.2
  96.2 1.3 collective-permute-start.1
  97.5 1.3 collective-permute-start.2
  99.4 3.7 collective-permute-done.2
  120.4 1.3 collective-permute-start.1
  121.7 1.3 collective-permute-start.2
  123.6 3.7 collective-permute-done.2
  144.7 1.3 collective-permute-start.1
  146.0 1.3 collective-permute-start.2
  147.9 4.8 %collective-permute-done.2 = f32[256]{0:T(256)S(1)} collective-permute-done((f32[256]{0:T(256)S(1)}, f32[256]{0:T(256)S(1)}, u32[]{:S(2)}, u32[]{:S(2)}) %collective-permute-start.2) | collective-permute-done | bytes 1056 | tf_op jit(solution)/shard_map/while/body/eval_jaxpr/ppermute | solution.py:40
  170.0 1.3 collective-permute-start.1
  171.3 1.3 collective-permute-start.2
  173.2 4.9 %collective-permute-done.2 = f32[256]{0:T(256)S(1)} collective-permute-done((f32[256]{0:T(256)S(1)}, f32[256]{0:T(256)S(1)}, u32[]{:S(2)}, u32[]{:S(2)}) %collective-permute-start.2) | collective-permute-done | bytes 1056 | tf_op jit(solution)/shard_map/while/body/eval_jaxpr/ppermute | solution.py:40
  195.4 1.3 collective-permute-start.1
  196.7 1.3 collective-permute-start.2
  198.6 4.9 %collective-permute-done.2 = f32[256]{0:T(256)S(1)} collective-permute-done((f32[256]{0:T(256)S(1)}, f32[256]{0:T(256)S(1)}, u32[]{:S(2)}, u32[]{:S(2)}) %collective-permute-start.2) | collective-permute-done | bytes 1056 | tf_op jit(solution)/shard_map/while/body/eval_jaxpr/ppermute | solution.py:40
  220.9 1.3 collective-permute-start.1
  222.2 1.3 collective-permute-start.2
  224.1 4.9 %collective-permute-done.2 = f32[256]{0:T(256)S(1)} collective-permute-done((f32[256]{0:T(256)S(1)}, f32[256]{0:T(256)S(1)}, u32[]{:S(2)}, u32[]{:S(2)}) %collective-permute-start.2) | collective-permute-done | bytes 1056 | tf_op jit(solution)/shard_map/while/body/eval_jaxpr/ppermute | solution.py:40
  246.3 1.3 collective-permute-start.1
  247.6 1.3 collective-permute-start.2
  249.5 4.9 %collective-permute-done.2 = f32[256]{0:T(256)S(1)} collective-permute-done((f32[256]{0:T(256)S(1)}, f32[256]{0:T(256)S(1)}, u32[]{:S(2)}, u32[]{:S(2)}) %collective-permute-start.2) | collective-permute-done | bytes 1056 | tf_op jit(solution)/shard_map/while/body/eval_jaxpr/ppermute | solution.py:40
  271.7 1.3 collective-permute-start.1
  273.0 1.3 collective-permute-start.2
  274.9 4.9 %collective-permute-done.2 = f32[256]{0:T(256)S(1)} collective-permute-done((f32[256]{0:T(256)S(1)}, f32[256]{0:T(256)S(1)}, u32[]{:S(2)}, u32[]{:S(2)}) %collective-permute-start.2) | collective-permute-done | bytes 1056 | tf_op jit(solution)/shard_map/while/body/eval_jaxpr/ppermute | solution.py:40
  297.1 1.3 collective-permute-start.1
  298.4 1.3 collective-permute-start.2
  300.3 4.9 %collective-permute-done.2 = f32[256]{0:T(256)S(1)} collective-permute-done((f32[256]{0:T(256)S(1)}, f32[256]{0:T(256)S(1)}, u32[]{:S(2)}, u32[]{:S(2)}) %collective-permute-start.2) | collective-permute-done | bytes 1056 | tf_op jit(solution)/shard_map/while/body/eval_jaxpr/ppermute | solution.py:40
  325.7 4.9 %collective-permute-done.2 = f32[256]{0:T(256)S(1)} collective-permute-done((f32[256]{0:T(256)S(1)}, f32[256]{0:T(256)S(1)}, u32[]{:S(2)}, u32[]{:S(2)}) %collective-permute-start.2) | collective-permute-done | bytes 1056 | tf_op jit(solution)/shard_map/while/body/eval_jaxpr/ppermute | solution.py:40
  351.1 4.9 %collective-permute-done.2 = f32[256]{0:T(256)S(1)} collective-permute-done((f32[256]{0:T(256)S(1)}, f32[256]{0:T(256)S(1)}, u32[]{:S(2)}, u32[]{:S(2)}) %collective-permute-start.2) | collective-permute-done | bytes 1056 | tf_op jit(solution)/shard_map/while/body/eval_jaxpr/ppermute | solution.py:40
  373.3 1.3 collective-permute-start.1
  374.6 1.3 collective-permute-start.2
  376.5 4.9 %collective-permute-done.2 = f32[256]{0:T(256)S(1)} collective-permute-done((f32[256]{0:T(256)S(1)}, f32[256]{0:T(256)S(1)}, u32[]{:S(2)}, u32[]{:S(2)}) %collective-permute-start.2) | collective-permute-done | bytes 1056 | tf_op jit(solution)/shard_map/while/body/eval_jaxpr/ppermute | solution.py:40
  401.9 4.9 %collective-permute-done.2 = f32[256]{0:T(256)S(1)} collective-permute-done((f32[256]{0:T(256)S(1)}, f32[256]{0:T(256)S(1)}, u32[]{:S(2)}, u32[]{:S(2)}) %collective-permute-start.2) | collective-permute-done | bytes 1056 | tf_op jit(solution)/shard_map/while/body/eval_jaxpr/ppermute | solution.py:40
  407.0 33.4 %all_to_all.16 = f32[32,1,400]{2,1,0:T(1,128)S(1)} all-to-all(f32[32,1,400]{2,1,0:T(1,128)S(1)} %reshape.905), channel_id=1, replica_groups=mesh['tm'=8,'paths'=32] {'paths'}, dimensions={0} | all-to-all | bytes 102400 | tf_op jit(solution)/shard_map/all_to_all | solution.py:18
  441.1 11.5 %all-to-all-start.2 = ((f32[8,1,2048]{2,1,0:T(1,128)}), f32[8,1,2048]{2,1,0:T(1,128)S(1)}, u32[]{:S(2)}, u32[]{:S(2)}) async-start(f32[8,1,2048]{2,1,0:T(1,128)} %broadcast_in_dim.459), calls=%async_computation.2 | async-start | bytes 131072 | tf_op jit(solution)/shard_map/all_to_all | solution.py:18
  454.7 5.2 %all-to-all-done.2 = f32[8,1,2048]{2,1,0:T(1,128)S(1)} async-done(((f32[8,1,2048]{2,1,0:T(1,128)}), f32[8,1,2048]{2,1,0:T(1,128)S(1)}, u32[]{:S(2)}, u32[]{:S(2)}) %all-to-all-start.2) | async-done | bytes 65568 | tf_op jit(solution)/shard_map/all_to_all | solution.py:18
  (1725 shorter events, 277.9 us)
Async XLA Ops:
  0.6 28.0 %collective-permute-start.3 = (f32[2048]{0:T(1024)}, f32[2048]{0:T(1024)S(1)}, u32[]{:S(2)}, u32[]{:S(2)}) collective-permute-start(f32[2048]{0:T(1024)} %bitcast.719), channel_id=1, source_target_pairs={{0,32},{32,64},{64,96},{96,128},{128,160},{160,192},{192,224},{1,3... | collective-permute-start | bytes 24584 | tf_op jit(solution)/shard_map/ppermute | solution.py:40
  5.0 23.7 %collective-permute-start.4 = (f32[80,2048]{1,0:T(8,128)}, f32[80,2048]{1,0:T(8,128)S(1)}, u32[]{:S(2)}, u32[]{:S(2)}) collective-permute-start(f32[80,2048]{1,0:T(8,128)} %bitcast.718), channel_id=1, source_target_pairs={{0,32},{32,64},{64,96},{96,128},{128,160},{160,192},{192,224},{1,3... | collective-permute-start | bytes 1966088 | tf_op jit(solution)/shard_map/ppermute | solution.py:40
  10.0 17.8 %all-to-all-start = ((f32[8,5,6]{1,2,0:T(8,128)}), f32[8,5,6]{1,2,0:T(8,128)S(1)}, u32[]{:S(2)}, u32[]{:S(2)}) async-start(f32[8,5,6]{1,2,0:T(8,128)} %broadcast_in_dim.457), calls=%async_computation | async-start | bytes 65536 | tf_op jit(solution)/shard_map/all_to_all | solution.py:18
  16.5 12.2 %collective-permute-start.5 = (f32[2048]{0:T(1024)S(1)}, f32[2048]{0:T(1024)S(1)}, u32[]{:S(2)}, u32[]{:S(2)}) collective-permute-start(f32[2048]{0:T(1024)S(1)} %bitcast.720), channel_id=1, source_target_pairs={{0,32},{32,64},{64,96},{96,128},{128,160},{160,192},{192,224},{1,3... | collective-permute-start | bytes 24584 | tf_op jit(solution)/shard_map/ppermute | solution.py:40
  46.2 8.2 %collective-permute-start = (f32[80,256]{1,0:T(8,128)S(1)}, f32[80,256]{1,0:T(8,128)S(1)}, u32[]{:S(2)}, u32[]{:S(2)}) collective-permute-start(f32[80,256]{1,0:T(8,128)S(1)} %get-tuple-element.1739), channel_id=1, source_target_pairs={{32,0},{64,32},{96,64},{128,96},{160,128},{192,160},{224,192},{33,... | collective-permute-start | bytes 245768 | tf_op jit(solution)/shard_map/while/body/eval_jaxpr/ppermute | solution.py:40
  47.5 6.9 %collective-permute-start.1 = (f32[256]{0:T(256)S(1)}, f32[256]{0:T(256)S(1)}, u32[]{:S(2)}, u32[]{:S(2)}) collective-permute-start(f32[256]{0:T(256)S(1)} %get-tuple-element.1740), channel_id=1, source_target_pairs={{32,0},{64,32},{96,64},{128,96},{160,128},{192,160},{224,192},{33,... | collective-permute-start | bytes 3080 | tf_op jit(solution)/shard_map/while/body/eval_jaxpr/ppermute | solution.py:40
  48.8 5.6 %collective-permute-start.2 = (f32[256]{0:T(256)S(1)}, f32[256]{0:T(256)S(1)}, u32[]{:S(2)}, u32[]{:S(2)}) collective-permute-start(f32[256]{0:T(256)S(1)} %get-tuple-element.1741), channel_id=1, source_target_pairs={{32,0},{64,32},{96,64},{128,96},{160,128},{192,160},{224,192},{33,... | collective-permute-start | bytes 3080 | tf_op jit(solution)/shard_map/while/body/eval_jaxpr/ppermute | solution.py:40
  70.4 8.5 %collective-permute-start = (f32[80,256]{1,0:T(8,128)S(1)}, f32[80,256]{1,0:T(8,128)S(1)}, u32[]{:S(2)}, u32[]{:S(2)}) collective-permute-start(f32[80,256]{1,0:T(8,128)S(1)} %get-tuple-element.1739), channel_id=1, source_target_pairs={{32,0},{64,32},{96,64},{128,96},{160,128},{192,160},{224,192},{33,... | collective-permute-start | bytes 245768 | tf_op jit(solution)/shard_map/while/body/eval_jaxpr/ppermute | solution.py:40
  71.7 7.2 %collective-permute-start.1 = (f32[256]{0:T(256)S(1)}, f32[256]{0:T(256)S(1)}, u32[]{:S(2)}, u32[]{:S(2)}) collective-permute-start(f32[256]{0:T(256)S(1)} %get-tuple-element.1740), channel_id=1, source_target_pairs={{32,0},{64,32},{96,64},{128,96},{160,128},{192,160},{224,192},{33,... | collective-permute-start | bytes 3080 | tf_op jit(solution)/shard_map/while/body/eval_jaxpr/ppermute | solution.py:40
  73.0 5.9 %collective-permute-start.2 = (f32[256]{0:T(256)S(1)}, f32[256]{0:T(256)S(1)}, u32[]{:S(2)}, u32[]{:S(2)}) collective-permute-start(f32[256]{0:T(256)S(1)} %get-tuple-element.1741), channel_id=1, source_target_pairs={{32,0},{64,32},{96,64},{128,96},{160,128},{192,160},{224,192},{33,... | collective-permute-start | bytes 3080 | tf_op jit(solution)/shard_map/while/body/eval_jaxpr/ppermute | solution.py:40
  94.9 8.2 %collective-permute-start = (f32[80,256]{1,0:T(8,128)S(1)}, f32[80,256]{1,0:T(8,128)S(1)}, u32[]{:S(2)}, u32[]{:S(2)}) collective-permute-start(f32[80,256]{1,0:T(8,128)S(1)} %get-tuple-element.1739), channel_id=1, source_target_pairs={{32,0},{64,32},{96,64},{128,96},{160,128},{192,160},{224,192},{33,... | collective-permute-start | bytes 245768 | tf_op jit(solution)/shard_map/while/body/eval_jaxpr/ppermute | solution.py:40
  96.2 6.9 %collective-permute-start.1 = (f32[256]{0:T(256)S(1)}, f32[256]{0:T(256)S(1)}, u32[]{:S(2)}, u32[]{:S(2)}) collective-permute-start(f32[256]{0:T(256)S(1)} %get-tuple-element.1740), channel_id=1, source_target_pairs={{32,0},{64,32},{96,64},{128,96},{160,128},{192,160},{224,192},{33,... | collective-permute-start | bytes 3080 | tf_op jit(solution)/shard_map/while/body/eval_jaxpr/ppermute | solution.py:40
  119.1 8.2 %collective-permute-start = (f32[80,256]{1,0:T(8,128)S(1)}, f32[80,256]{1,0:T(8,128)S(1)}, u32[]{:S(2)}, u32[]{:S(2)}) collective-permute-start(f32[80,256]{1,0:T(8,128)S(1)} %get-tuple-element.1739), channel_id=1, source_target_pairs={{32,0},{64,32},{96,64},{128,96},{160,128},{192,160},{224,192},{33,... | collective-permute-start | bytes 245768 | tf_op jit(solution)/shard_map/while/body/eval_jaxpr/ppermute | solution.py:40
  120.4 6.9 %collective-permute-start.1 = (f32[256]{0:T(256)S(1)}, f32[256]{0:T(256)S(1)}, u32[]{:S(2)}, u32[]{:S(2)}) collective-permute-start(f32[256]{0:T(256)S(1)} %get-tuple-element.1740), channel_id=1, source_target_pairs={{32,0},{64,32},{96,64},{128,96},{160,128},{192,160},{224,192},{33,... | collective-permute-start | bytes 3080 | tf_op jit(solution)/shard_map/while/body/eval_jaxpr/ppermute | solution.py:40
  143.4 9.3 %collective-permute-start = (f32[80,256]{1,0:T(8,128)S(1)}, f32[80,256]{1,0:T(8,128)S(1)}, u32[]{:S(2)}, u32[]{:S(2)}) collective-permute-start(f32[80,256]{1,0:T(8,128)S(1)} %get-tuple-element.1739), channel_id=1, source_target_pairs={{32,0},{64,32},{96,64},{128,96},{160,128},{192,160},{224,192},{33,... | collective-permute-start | bytes 245768 | tf_op jit(solution)/shard_map/while/body/eval_jaxpr/ppermute | solution.py:40
  144.7 8.0 %collective-permute-start.1 = (f32[256]{0:T(256)S(1)}, f32[256]{0:T(256)S(1)}, u32[]{:S(2)}, u32[]{:S(2)}) collective-permute-start(f32[256]{0:T(256)S(1)} %get-tuple-element.1740), channel_id=1, source_target_pairs={{32,0},{64,32},{96,64},{128,96},{160,128},{192,160},{224,192},{33,... | collective-permute-start | bytes 3080 | tf_op jit(solution)/shard_map/while/body/eval_jaxpr/ppermute | solution.py:40
  146.0 6.7 %collective-permute-start.2 = (f32[256]{0:T(256)S(1)}, f32[256]{0:T(256)S(1)}, u32[]{:S(2)}, u32[]{:S(2)}) collective-permute-start(f32[256]{0:T(256)S(1)} %get-tuple-element.1741), channel_id=1, source_target_pairs={{32,0},{64,32},{96,64},{128,96},{160,128},{192,160},{224,192},{33,... | collective-permute-start | bytes 3080 | tf_op jit(solution)/shard_map/while/body/eval_jaxpr/ppermute | solution.py:40
  168.7 9.4 %collective-permute-start = (f32[80,256]{1,0:T(8,128)S(1)}, f32[80,256]{1,0:T(8,128)S(1)}, u32[]{:S(2)}, u32[]{:S(2)}) collective-permute-start(f32[80,256]{1,0:T(8,128)S(1)} %get-tuple-element.1739), channel_id=1, source_target_pairs={{32,0},{64,32},{96,64},{128,96},{160,128},{192,160},{224,192},{33,... | collective-permute-start | bytes 245768 | tf_op jit(solution)/shard_map/while/body/eval_jaxpr/ppermute | solution.py:40
  170.0 8.1 %collective-permute-start.1 = (f32[256]{0:T(256)S(1)}, f32[256]{0:T(256)S(1)}, u32[]{:S(2)}, u32[]{:S(2)}) collective-permute-start(f32[256]{0:T(256)S(1)} %get-tuple-element.1740), channel_id=1, source_target_pairs={{32,0},{64,32},{96,64},{128,96},{160,128},{192,160},{224,192},{33,... | collective-permute-start | bytes 3080 | tf_op jit(solution)/shard_map/while/body/eval_jaxpr/ppermute | solution.py:40
  171.3 6.8 %collective-permute-start.2 = (f32[256]{0:T(256)S(1)}, f32[256]{0:T(256)S(1)}, u32[]{:S(2)}, u32[]{:S(2)}) collective-permute-start(f32[256]{0:T(256)S(1)} %get-tuple-element.1741), channel_id=1, source_target_pairs={{32,0},{64,32},{96,64},{128,96},{160,128},{192,160},{224,192},{33,... | collective-permute-start | bytes 3080 | tf_op jit(solution)/shard_map/while/body/eval_jaxpr/ppermute | solution.py:40
  194.1 9.4 %collective-permute-start = (f32[80,256]{1,0:T(8,128)S(1)}, f32[80,256]{1,0:T(8,128)S(1)}, u32[]{:S(2)}, u32[]{:S(2)}) collective-permute-start(f32[80,256]{1,0:T(8,128)S(1)} %get-tuple-element.1739), channel_id=1, source_target_pairs={{32,0},{64,32},{96,64},{128,96},{160,128},{192,160},{224,192},{33,... | collective-permute-start | bytes 245768 | tf_op jit(solution)/shard_map/while/body/eval_jaxpr/ppermute | solution.py:40
  195.4 8.1 %collective-permute-start.1 = (f32[256]{0:T(256)S(1)}, f32[256]{0:T(256)S(1)}, u32[]{:S(2)}, u32[]{:S(2)}) collective-permute-start(f32[256]{0:T(256)S(1)} %get-tuple-element.1740), channel_id=1, source_target_pairs={{32,0},{64,32},{96,64},{128,96},{160,128},{192,160},{224,192},{33,... | collective-permute-start | bytes 3080 | tf_op jit(solution)/shard_map/while/body/eval_jaxpr/ppermute | solution.py:40
  196.7 6.8 %collective-permute-start.2 = (f32[256]{0:T(256)S(1)}, f32[256]{0:T(256)S(1)}, u32[]{:S(2)}, u32[]{:S(2)}) collective-permute-start(f32[256]{0:T(256)S(1)} %get-tuple-element.1741), channel_id=1, source_target_pairs={{32,0},{64,32},{96,64},{128,96},{160,128},{192,160},{224,192},{33,... | collective-permute-start | bytes 3080 | tf_op jit(solution)/shard_map/while/body/eval_jaxpr/ppermute | solution.py:40
  219.6 9.4 %collective-permute-start = (f32[80,256]{1,0:T(8,128)S(1)}, f32[80,256]{1,0:T(8,128)S(1)}, u32[]{:S(2)}, u32[]{:S(2)}) collective-permute-start(f32[80,256]{1,0:T(8,128)S(1)} %get-tuple-element.1739), channel_id=1, source_target_pairs={{32,0},{64,32},{96,64},{128,96},{160,128},{192,160},{224,192},{33,... | collective-permute-start | bytes 245768 | tf_op jit(solution)/shard_map/while/body/eval_jaxpr/ppermute | solution.py:40
  220.9 8.1 %collective-permute-start.1 = (f32[256]{0:T(256)S(1)}, f32[256]{0:T(256)S(1)}, u32[]{:S(2)}, u32[]{:S(2)}) collective-permute-start(f32[256]{0:T(256)S(1)} %get-tuple-element.1740), channel_id=1, source_target_pairs={{32,0},{64,32},{96,64},{128,96},{160,128},{192,160},{224,192},{33,... | collective-permute-start | bytes 3080 | tf_op jit(solution)/shard_map/while/body/eval_jaxpr/ppermute | solution.py:40
  222.2 6.8 %collective-permute-start.2 = (f32[256]{0:T(256)S(1)}, f32[256]{0:T(256)S(1)}, u32[]{:S(2)}, u32[]{:S(2)}) collective-permute-start(f32[256]{0:T(256)S(1)} %get-tuple-element.1741), channel_id=1, source_target_pairs={{32,0},{64,32},{96,64},{128,96},{160,128},{192,160},{224,192},{33,... | collective-permute-start | bytes 3080 | tf_op jit(solution)/shard_map/while/body/eval_jaxpr/ppermute | solution.py:40
  245.0 9.4 %collective-permute-start = (f32[80,256]{1,0:T(8,128)S(1)}, f32[80,256]{1,0:T(8,128)S(1)}, u32[]{:S(2)}, u32[]{:S(2)}) collective-permute-start(f32[80,256]{1,0:T(8,128)S(1)} %get-tuple-element.1739), channel_id=1, source_target_pairs={{32,0},{64,32},{96,64},{128,96},{160,128},{192,160},{224,192},{33,... | collective-permute-start | bytes 245768 | tf_op jit(solution)/shard_map/while/body/eval_jaxpr/ppermute | solution.py:40
  246.3 8.1 %collective-permute-start.1 = (f32[256]{0:T(256)S(1)}, f32[256]{0:T(256)S(1)}, u32[]{:S(2)}, u32[]{:S(2)}) collective-permute-start(f32[256]{0:T(256)S(1)} %get-tuple-element.1740), channel_id=1, source_target_pairs={{32,0},{64,32},{96,64},{128,96},{160,128},{192,160},{224,192},{33,... | collective-permute-start | bytes 3080 | tf_op jit(solution)/shard_map/while/body/eval_jaxpr/ppermute | solution.py:40
  247.6 6.8 %collective-permute-start.2 = (f32[256]{0:T(256)S(1)}, f32[256]{0:T(256)S(1)}, u32[]{:S(2)}, u32[]{:S(2)}) collective-permute-start(f32[256]{0:T(256)S(1)} %get-tuple-element.1741), channel_id=1, source_target_pairs={{32,0},{64,32},{96,64},{128,96},{160,128},{192,160},{224,192},{33,... | collective-permute-start | bytes 3080 | tf_op jit(solution)/shard_map/while/body/eval_jaxpr/ppermute | solution.py:40
  270.4 9.4 %collective-permute-start = (f32[80,256]{1,0:T(8,128)S(1)}, f32[80,256]{1,0:T(8,128)S(1)}, u32[]{:S(2)}, u32[]{:S(2)}) collective-permute-start(f32[80,256]{1,0:T(8,128)S(1)} %get-tuple-element.1739), channel_id=1, source_target_pairs={{32,0},{64,32},{96,64},{128,96},{160,128},{192,160},{224,192},{33,... | collective-permute-start | bytes 245768 | tf_op jit(solution)/shard_map/while/body/eval_jaxpr/ppermute | solution.py:40
  271.7 8.1 %collective-permute-start.1 = (f32[256]{0:T(256)S(1)}, f32[256]{0:T(256)S(1)}, u32[]{:S(2)}, u32[]{:S(2)}) collective-permute-start(f32[256]{0:T(256)S(1)} %get-tuple-element.1740), channel_id=1, source_target_pairs={{32,0},{64,32},{96,64},{128,96},{160,128},{192,160},{224,192},{33,... | collective-permute-start | bytes 3080 | tf_op jit(solution)/shard_map/while/body/eval_jaxpr/ppermute | solution.py:40
  273.0 6.8 %collective-permute-start.2 = (f32[256]{0:T(256)S(1)}, f32[256]{0:T(256)S(1)}, u32[]{:S(2)}, u32[]{:S(2)}) collective-permute-start(f32[256]{0:T(256)S(1)} %get-tuple-element.1741), channel_id=1, source_target_pairs={{32,0},{64,32},{96,64},{128,96},{160,128},{192,160},{224,192},{33,... | collective-permute-start | bytes 3080 | tf_op jit(solution)/shard_map/while/body/eval_jaxpr/ppermute | solution.py:40
  295.8 9.4 %collective-permute-start = (f32[80,256]{1,0:T(8,128)S(1)}, f32[80,256]{1,0:T(8,128)S(1)}, u32[]{:S(2)}, u32[]{:S(2)}) collective-permute-start(f32[80,256]{1,0:T(8,128)S(1)} %get-tuple-element.1739), channel_id=1, source_target_pairs={{32,0},{64,32},{96,64},{128,96},{160,128},{192,160},{224,192},{33,... | collective-permute-start | bytes 245768 | tf_op jit(solution)/shard_map/while/body/eval_jaxpr/ppermute | solution.py:40
  297.1 8.1 %collective-permute-start.1 = (f32[256]{0:T(256)S(1)}, f32[256]{0:T(256)S(1)}, u32[]{:S(2)}, u32[]{:S(2)}) collective-permute-start(f32[256]{0:T(256)S(1)} %get-tuple-element.1740), channel_id=1, source_target_pairs={{32,0},{64,32},{96,64},{128,96},{160,128},{192,160},{224,192},{33,... | collective-permute-start | bytes 3080 | tf_op jit(solution)/shard_map/while/body/eval_jaxpr/ppermute | solution.py:40
  298.4 6.8 %collective-permute-start.2 = (f32[256]{0:T(256)S(1)}, f32[256]{0:T(256)S(1)}, u32[]{:S(2)}, u32[]{:S(2)}) collective-permute-start(f32[256]{0:T(256)S(1)} %get-tuple-element.1741), channel_id=1, source_target_pairs={{32,0},{64,32},{96,64},{128,96},{160,128},{192,160},{224,192},{33,... | collective-permute-start | bytes 3080 | tf_op jit(solution)/shard_map/while/body/eval_jaxpr/ppermute | solution.py:40
  321.2 9.4 %collective-permute-start = (f32[80,256]{1,0:T(8,128)S(1)}, f32[80,256]{1,0:T(8,128)S(1)}, u32[]{:S(2)}, u32[]{:S(2)}) collective-permute-start(f32[80,256]{1,0:T(8,128)S(1)} %get-tuple-element.1739), channel_id=1, source_target_pairs={{32,0},{64,32},{96,64},{128,96},{160,128},{192,160},{224,192},{33,... | collective-permute-start | bytes 245768 | tf_op jit(solution)/shard_map/while/body/eval_jaxpr/ppermute | solution.py:40
  322.5 8.1 %collective-permute-start.1 = (f32[256]{0:T(256)S(1)}, f32[256]{0:T(256)S(1)}, u32[]{:S(2)}, u32[]{:S(2)}) collective-permute-start(f32[256]{0:T(256)S(1)} %get-tuple-element.1740), channel_id=1, source_target_pairs={{32,0},{64,32},{96,64},{128,96},{160,128},{192,160},{224,192},{33,... | collective-permute-start | bytes 3080 | tf_op jit(solution)/shard_map/while/body/eval_jaxpr/ppermute | solution.py:40
  323.8 6.8 %collective-permute-start.2 = (f32[256]{0:T(256)S(1)}, f32[256]{0:T(256)S(1)}, u32[]{:S(2)}, u32[]{:S(2)}) collective-permute-start(f32[256]{0:T(256)S(1)} %get-tuple-element.1741), channel_id=1, source_target_pairs={{32,0},{64,32},{96,64},{128,96},{160,128},{192,160},{224,192},{33,... | collective-permute-start | bytes 3080 | tf_op jit(solution)/shard_map/while/body/eval_jaxpr/ppermute | solution.py:40
  346.6 9.4 %collective-permute-start = (f32[80,256]{1,0:T(8,128)S(1)}, f32[80,256]{1,0:T(8,128)S(1)}, u32[]{:S(2)}, u32[]{:S(2)}) collective-permute-start(f32[80,256]{1,0:T(8,128)S(1)} %get-tuple-element.1739), channel_id=1, source_target_pairs={{32,0},{64,32},{96,64},{128,96},{160,128},{192,160},{224,192},{33,... | collective-permute-start | bytes 245768 | tf_op jit(solution)/shard_map/while/body/eval_jaxpr/ppermute | solution.py:40
  347.9 8.1 %collective-permute-start.1 = (f32[256]{0:T(256)S(1)}, f32[256]{0:T(256)S(1)}, u32[]{:S(2)}, u32[]{:S(2)}) collective-permute-start(f32[256]{0:T(256)S(1)} %get-tuple-element.1740), channel_id=1, source_target_pairs={{32,0},{64,32},{96,64},{128,96},{160,128},{192,160},{224,192},{33,... | collective-permute-start | bytes 3080 | tf_op jit(solution)/shard_map/while/body/eval_jaxpr/ppermute | solution.py:40
  349.2 6.8 %collective-permute-start.2 = (f32[256]{0:T(256)S(1)}, f32[256]{0:T(256)S(1)}, u32[]{:S(2)}, u32[]{:S(2)}) collective-permute-start(f32[256]{0:T(256)S(1)} %get-tuple-element.1741), channel_id=1, source_target_pairs={{32,0},{64,32},{96,64},{128,96},{160,128},{192,160},{224,192},{33,... | collective-permute-start | bytes 3080 | tf_op jit(solution)/shard_map/while/body/eval_jaxpr/ppermute | solution.py:40
  372.0 9.4 %collective-permute-start = (f32[80,256]{1,0:T(8,128)S(1)}, f32[80,256]{1,0:T(8,128)S(1)}, u32[]{:S(2)}, u32[]{:S(2)}) collective-permute-start(f32[80,256]{1,0:T(8,128)S(1)} %get-tuple-element.1739), channel_id=1, source_target_pairs={{32,0},{64,32},{96,64},{128,96},{160,128},{192,160},{224,192},{33,... | collective-permute-start | bytes 245768 | tf_op jit(solution)/shard_map/while/body/eval_jaxpr/ppermute | solution.py:40
  373.3 8.1 %collective-permute-start.1 = (f32[256]{0:T(256)S(1)}, f32[256]{0:T(256)S(1)}, u32[]{:S(2)}, u32[]{:S(2)}) collective-permute-start(f32[256]{0:T(256)S(1)} %get-tuple-element.1740), channel_id=1, source_target_pairs={{32,0},{64,32},{96,64},{128,96},{160,128},{192,160},{224,192},{33,... | collective-permute-start | bytes 3080 | tf_op jit(solution)/shard_map/while/body/eval_jaxpr/ppermute | solution.py:40
  374.6 6.8 %collective-permute-start.2 = (f32[256]{0:T(256)S(1)}, f32[256]{0:T(256)S(1)}, u32[]{:S(2)}, u32[]{:S(2)}) collective-permute-start(f32[256]{0:T(256)S(1)} %get-tuple-element.1741), channel_id=1, source_target_pairs={{32,0},{64,32},{96,64},{128,96},{160,128},{192,160},{224,192},{33,... | collective-permute-start | bytes 3080 | tf_op jit(solution)/shard_map/while/body/eval_jaxpr/ppermute | solution.py:40
  397.5 9.4 %collective-permute-start = (f32[80,256]{1,0:T(8,128)S(1)}, f32[80,256]{1,0:T(8,128)S(1)}, u32[]{:S(2)}, u32[]{:S(2)}) collective-permute-start(f32[80,256]{1,0:T(8,128)S(1)} %get-tuple-element.1739), channel_id=1, source_target_pairs={{32,0},{64,32},{96,64},{128,96},{160,128},{192,160},{224,192},{33,... | collective-permute-start | bytes 245768 | tf_op jit(solution)/shard_map/while/body/eval_jaxpr/ppermute | solution.py:40
  398.8 8.1 %collective-permute-start.1 = (f32[256]{0:T(256)S(1)}, f32[256]{0:T(256)S(1)}, u32[]{:S(2)}, u32[]{:S(2)}) collective-permute-start(f32[256]{0:T(256)S(1)} %get-tuple-element.1740), channel_id=1, source_target_pairs={{32,0},{64,32},{96,64},{128,96},{160,128},{192,160},{224,192},{33,... | collective-permute-start | bytes 3080 | tf_op jit(solution)/shard_map/while/body/eval_jaxpr/ppermute | solution.py:40
  400.1 6.8 %collective-permute-start.2 = (f32[256]{0:T(256)S(1)}, f32[256]{0:T(256)S(1)}, u32[]{:S(2)}, u32[]{:S(2)}) collective-permute-start(f32[256]{0:T(256)S(1)} %get-tuple-element.1741), channel_id=1, source_target_pairs={{32,0},{64,32},{96,64},{128,96},{160,128},{192,160},{224,192},{33,... | collective-permute-start | bytes 3080 | tf_op jit(solution)/shard_map/while/body/eval_jaxpr/ppermute | solution.py:40
  441.1 18.8 %all-to-all-start.2 = ((f32[8,1,2048]{2,1,0:T(1,128)}), f32[8,1,2048]{2,1,0:T(1,128)S(1)}, u32[]{:S(2)}, u32[]{:S(2)}) async-start(f32[8,1,2048]{2,1,0:T(1,128)} %broadcast_in_dim.459), calls=%async_computation.2 | async-start | bytes 131072 | tf_op jit(solution)/shard_map/all_to_all | solution.py:18
  (8 other events, 31.7 us)
where the time goes:
time: 465 us; the launch traced here: 461 us
  matrix products  198 us (43%)
  starting transfers between devices  87.4 us (19%)
  waiting for transfers between devices  81 us (17%)
  other arithmetic  43 us (9%)
  blocking collectives  33.4 us (7%)
  local copies, waits for them, and re-layouts  9.65 us (2%)
  loops' own time  6.87 us (1%)
    dot_general x75, matrix products, segment(): jnp.einsum('fi,fp->ip', factor_loads, shock_rows[offset_date], precision=...  75.7 us
    ppermute x48, starting transfers between devices, passed_along(): lax.ppermute(value, axis, [(source, source + steps) for source in range(i...  69.4 us
    ppermute x48, waiting for transfers between devices, passed_along(): lax.ppermute(value, axis, [(source, source + steps) for source in range(i...  68.8 us
    dot_general x150, matrix products, segment(): jnp.einsum('ij,fjp->fip', triangle, factor_loads[:, :, None] * scaled[Non...  60.2 us
    dot_general x150, matrix products, segment(): jnp.dot(triangle, living[:, None] * jnp.log1p(ACCRUAL * current), precisi...  52.5 us
    all_to_all x1, blocking collectives, copy_for_each(): return lax.all_to_all(copies, axis, split_axis=0, concat_axis=0, tiled=True)  33.4 us
    all_to_all x2, starting transfers between devices, copy_for_each(): return lax.all_to_all(copies, axis, split_axis=0, concat_axis=0, tiled=True)  18 us
    all_to_all x2, waiting for transfers between devices, copy_for_each(): return lax.all_to_all(copies, axis, split_axis=0, concat_axis=0, tiled=True)  12.1 us
  transfers between devices with their start and end apart: 50, of which 17 were waited for; matrix products, arithmetic and copies ran while one was open for 3% of the time, Pallas kernels for 0%

commit v1 on v0

v1 whole, which is shorter than its diff:
```python
import functools

import jax
import jax.numpy as jnp
from jax import lax
from jax.experimental import pallas as pl
from jax.experimental.pallas import tpu as pltpu
from jax.sharding import PartitionSpec as P

ACCRUAL = 0.25
STRIKE = 0.04
SMOOTHING = 0.01
NOTIONAL = 100.0
HIGHEST = lax.Precision.HIGHEST
MESH = pl.DeviceIdType.MESH
F32 = jnp.float32
BF16 = jnp.bfloat16

SHARDS = 8
PER = 5
NF = 80
VMEM_LIMIT = 60 * 1024 * 1024


def first_needed(shard):
    return max(2 * shard * PER - 1, 0)


def row_start(shard):
    return first_needed(shard) // 16 * 16


def sent_start(shard):
    return first_needed(shard) // 8 * 8


def exchange_kernel(
    width,
    shocks, bits, rates, numer, survive, vols, regress, slots,
    shocks_x, bits_x, rates_x, numer_x, survive_x, vols_x, regress_x, slots_x,
    send_sem, recv_sem, local_sem,
):
    me = lax.axis_index("tm")
    barrier = pltpu.get_barrier_semaphore()
    for step in range(1, SHARDS):
        other = lax.rem(me + step, SHARDS)
        pl.semaphore_signal(barrier, inc=1, device_id={"tm": other}, device_id_type=MESH)
    pl.semaphore_wait(barrier, SHARDS - 1)

    def cut(target):
        return pl.ds(pl.multiple_of(target * width, width), width)

    def pairs(source, target):
        return (
            (vols, vols_x.at[source]),
            (regress, regress_x.at[source]),
            (slots, slots_x.at[source]),
            (numer.at[:, cut(target)], numer_x.at[source]),
            (survive.at[:, cut(target)], survive_x.at[source]),
            (bits.at[:, cut(target)], bits_x.at[source]),
            (shocks.at[:, :, cut(target)], shocks_x.at[source]),
        )

    def rate_pair(source, target):
        top = sent_start(source + 1)
        rows = pl.ds(top, NF - top)
        return (rates.at[0, rows, cut(target)], rates_x.at[source, rows, :])

    def remote(pair, kind, source, step, target):
        return pltpu.make_async_remote_copy(
            src_ref=pair[0],
            dst_ref=pair[1],
            send_sem=send_sem.at[kind, step],
            recv_sem=recv_sem.at[kind, source],
            device_id={"tm": target},
            device_id_type=MESH,
        )

    order = (4, 3, 5, 2, 6, 1, 7)
    for step in order:
        target = lax.rem(me + step, SHARDS)
        for kind, pair in enumerate(pairs(me, target)):
            remote(pair, kind, me, step, target).start()
    for source in range(SHARDS - 1):

        @pl.when(me == source)
        def _():
            for step in order:
                target = lax.rem(me + step, SHARDS)
                remote(rate_pair(source, target), 7, source, step, target).start()

    for kind, pair in enumerate(pairs(me, me)):
        pltpu.make_async_copy(pair[0], pair[1], local_sem.at[kind]).start()
    for source in range(SHARDS - 1):

        @pl.when(me == source)
        def _():
            pair = rate_pair(source, source)
            pltpu.make_async_copy(pair[0], pair[1], local_sem.at[7]).start()

    for kind, pair in enumerate(pairs(me, me)):
        pltpu.make_async_copy(pair[0], pair[1], local_sem.at[kind]).wait()
    for source in range(SHARDS - 1):

        @pl.when(me == source)
        def _():
            pair = rate_pair(source, source)
            pltpu.make_async_copy(pair[0], pair[1], local_sem.at[7]).wait()

    for step in order:
        target = lax.rem(me + step, SHARDS)
        for kind, pair in enumerate(pairs(me, target)):
            remote(pair, kind, me, step, target).wait_send()
    for source in range(SHARDS - 1):

        @pl.when(me == source)
        def _():
            for step in order:
                target = lax.rem(me + step, SHARDS)
                remote(rate_pair(source, target), 7, source, step, target).wait_send()

    for source in range(SHARDS):

        @pl.when(me != source)
        def _():
            for kind, pair in enumerate(pairs(source, source)):
                remote(pair, kind, source, 0, source).wait_recv()
            if source < SHARDS - 1:
                remote(rate_pair(source, source), 7, source, 0, source).wait_recv()


def exchange(width, shocks, bits, rates, numer, survive, vols, regress, slots):
    anywhere = pl.BlockSpec(memory_space=pl.ANY)
    shapes = (
        ((SHARDS, PER, 4, width), F32),
        ((SHARDS, PER, width), jnp.int32),
        ((SHARDS, NF, width), F32),
        ((SHARDS, 1, width), F32),
        ((SHARDS, 1, width), F32),
        ((SHARDS, PER, NF), F32),
        ((SHARDS, PER, 6), F32),
        ((SHARDS, 1, PER), jnp.int32),
    )
    return pl.pallas_call(
        functools.partial(exchange_kernel, width),
        name="exchange",
        out_shape=[jax.ShapeDtypeStruct(s, t) for s, t in shapes],
        in_specs=[anywhere] * 8,
        out_specs=[anywhere] * 8,
        scratch_shapes=[
            pltpu.SemaphoreType.DMA((8, SHARDS)),
            pltpu.SemaphoreType.DMA((8, SHARDS)),
            pltpu.SemaphoreType.DMA((8,)),
        ],
        compiler_params=pltpu.CompilerParams(
            collective_id=0, has_side_effects=True, vmem_limit_bytes=VMEM_LIMIT
        ),
    )(shocks, bits, rates, numer, survive, vols, regress, slots)


def halves(x):
    high = x.astype(BF16)
    low = (x - high.astype(F32)).astype(BF16)
    return high, low


def compute_kernel(
    path_weight,
    curve, loads, shocks, bits, rates, numer, survive, vols, regress, slots,
    vega, value,
    square, stack, forward_lhs, backward_lhs, sums_lhs, tails_lhs, sigma, curve_wide,
    state, start, v_all, w_all, tail_all, annuity_all, last_all, growth_all, flags,
    mult_tail, mult_last, mult_numer, columns,
):
    width = value.shape[1]
    a = ACCRUAL

    def wide(x):
        return jnp.concatenate([x] * (width // 128), axis=1)

    lane = lax.broadcasted_iota(jnp.int32, (128, 128), 1)
    row = lax.broadcasted_iota(jnp.int32, (128, 128), 0)
    square[...] = jnp.zeros((128, 128), F32)
    raw = loads[...]
    unit = raw / jnp.sqrt(jnp.sum(raw * raw, axis=0, keepdims=True))
    square[0:4, 0:NF] = unit
    padded = square[...]
    turned = jnp.transpose(padded)
    full = jnp.dot(turned, padded, precision=HIGHEST, preferred_element_type=F32)

    def split_f32(x):
        high = x.astype(BF16).astype(F32)
        return high, (x - high).astype(BF16).astype(F32)

    for target, keep in ((forward_lhs, row <= lane), (backward_lhs, row >= lane)):
        high, low = split_f32(jnp.where(keep, full, 0.0))
        stack[...] = jnp.zeros((256, 128), F32)
        stack[0:NF, :] = high[:NF]
        stack[NF : 2 * NF, :] = high[:NF]
        stack[2 * NF : 3 * NF, :] = low[:NF]
        if target is forward_lhs:
            part_high, part_low = split_f32(padded)
            stack[240:244, :] = part_high[0:4]
            stack[244:248, :] = part_high[0:4]
            stack[248:252, :] = part_low[0:4]
        target[...] = jnp.transpose(stack[...])[:NF].astype(BF16)
    stack[...] = jnp.zeros((256, 128), F32)
    lower = jnp.where((row <= lane) & (row < NF), 1.0, 0.0)
    stack[0:NF, :] = lower[:NF]
    stack[NF : 2 * NF, :] = lower[:NF]
    sums_lhs[...] = jnp.transpose(stack[...])[:NF].astype(BF16)
    upper = jnp.where((row >= lane) & (row < NF), 1.0, 0.0)
    stack[0:NF, :] = upper[:NF]
    stack[NF : 2 * NF, :] = upper[:NF]
    tails_lhs[...] = jnp.transpose(stack[...])[:NF].astype(BF16)

    square[...] = jnp.zeros((128, 128), F32)
    for s in range(SHARDS):
        square[s * PER : (s + 1) * PER, 0:NF] = vols[s]
    turned = jnp.transpose(square[...])
    for s in range(SHARDS):
        top = row_start(s)
        for k in range(PER):
            d = s * PER + k
            column = jnp.broadcast_to(turned[top:NF, d : d + 1], (NF - top, 128))
            sigma[s, k, top:NF, :] = jnp.where(row[top:NF] >= 2 * d + 1, column, 0.0)
    square[...] = jnp.zeros((128, 128), F32)
    square[0:1, 0:NF] = curve[...]
    column = jnp.transpose(square[...])[:NF, 0:1]
    curve_wide[...] = jnp.broadcast_to(column, (NF, 128))

    square[...] = jnp.zeros((128, 128), F32)
    for s in range(SHARDS):
        square[s * PER : (s + 1) * PER, 0:6] = regress[s]
    ids = jnp.concatenate([slots[s] for s in range(SHARDS)], axis=0)
    hot = jnp.concatenate(
        [
            jnp.where(jnp.broadcast_to(ids[:, k : k + 1], (SHARDS, 128)) == lane[:SHARDS], 1.0, 0.0)
            for k in range(PER)
        ],
        axis=0,
    )
    weights = jnp.dot(hot, square[...], precision=HIGHEST, preferred_element_type=F32)

    for s in range(SHARDS):
        for k in range(PER):
            flags[k, s : s + 1, :] = bits[s, k : k + 1, :].astype(F32)

    for s in range(SHARDS):
        top = row_start(s)
        if s == 0:
            first = wide(curve_wide[...])
        else:
            position = lax.broadcasted_iota(jnp.int32, (NF - top, width), 0) + top
            first = jnp.where(position >= first_needed(s), rates[s - 1, top:NF, :], STRIKE)
        start[s, top:NF, :] = first
        state[s, top:NF, :] = first

    def zeros_above(top, x):
        if top == 0:
            return x
        return jnp.concatenate([jnp.zeros((top, x.shape[1]), x.dtype), x], axis=0)

    def forward(k, carry):
        for s in range(SHARDS):
            top = row_start(s)
            if s == 0:
                h = jnp.where(k == 0, a, 2.0 * a).astype(F32)
                root = jnp.where(k == 0, a**0.5, (2.0 * a) ** 0.5).astype(F32)
            else:
                h, root = 2.0 * a, (2.0 * a) ** 0.5
            current = state[s, top:NF, :]
            scaled = a * current
            v = scaled / (1.0 + scaled)
            v_all[s, k, top:NF, :] = v
            opening = 2 * (s * PER + k)
            second = 1.0 + a * state[s, pl.ds(opening, 1), :]
            if s == 0:
                before = 1.0 + a * state[s, pl.ds(jnp.maximum(opening - 1, 0), 1), :]
                before = jnp.where(k == 0, 1.0, before)
            else:
                before = 1.0 + a * state[s, pl.ds(opening - 1, 1), :]
            growth_all[k, s : s + 1, :] = before * second
            sig = wide(sigma[s, k, top:NF, :])
            hsig = h * sig
            high, low = halves(hsig * v)
            shock = root * shocks[s, k]
            shock_high = shock.astype(BF16).astype(F32)
            noise = jnp.concatenate(
                [shock_high, shock - shock_high, shock_high, jnp.zeros_like(shock)], axis=0
            ).astype(BF16)
            high, low = zeros_above(top, high), zeros_above(top, low)
            rhs = jnp.concatenate([high, low, high, noise], axis=0)
            w = jnp.dot(forward_lhs[top:NF, :], rhs, preferred_element_type=F32)
            w_all[s, k, top:NF, :] = w - hsig
            current = current * jnp.exp(sig * (w - 0.5 * hsig))
            state[s, top:NF, :] = current
            position = lax.broadcasted_iota(jnp.int32, (NF - top, width), 0) + top
            living = position > opening
            logs = jnp.where(living, jnp.log(1.0 + a * current), 0.0)
            high, low = halves(logs)
            rhs = jnp.concatenate([zeros_above(top, high), zeros_above(top, low)], axis=0)
            total = jnp.dot(sums_lhs[top:NF, 0 : 2 * NF], rhs, preferred_element_type=F32)
            bonds = jnp.where(living, jnp.exp(-total), 0.0)
            annuity_all[k, s : s + 1, :] = a * jnp.sum(bonds, axis=0, keepdims=True)
            last_all[k, s : s + 1, :] = bonds[NF - top - 1 : NF - top]
            high, low = halves(bonds)
            rhs = jnp.concatenate([zeros_above(top, high), zeros_above(top, low)], axis=0)
            tail_all[s, k, top:NF, :] = jnp.dot(
                tails_lhs[top:NF, 0 : 2 * NF], rhs, preferred_element_type=F32
            )
        return carry

    lax.fori_loop(0, PER, forward, 0)
    for s in range(SHARDS):
        top = row_start(s)
        scaled = a * state[s, top:NF, :]
        v_all[s, PER, top:NF, :] = scaled / (1.0 + scaled)

    one = jnp.ones((1, width), F32)
    numeraire = jnp.concatenate([one] + [numer[s] for s in range(SHARDS - 1)], axis=0)
    survival = jnp.concatenate([one] + [survive[s] for s in range(SHARDS - 1)], axis=0)
    scale = path_weight * NOTIONAL
    kept = []
    values = jnp.zeros((SHARDS, width), F32)
    for k in range(PER):
        numeraire = numeraire * growth_all[k]
        annuity = annuity_all[k]
        floating = 1.0 - last_all[k]
        exercise = floating - STRIKE * annuity
        inverse = 1.0 / annuity
        money = (floating * inverse - STRIKE) / SMOOTHING
        w = [
            jnp.broadcast_to(weights[k * SHARDS : (k + 1) * SHARDS, b : b + 1], (SHARDS, width))
            for b in range(6)
        ]
        slope = w[3] + money * (w[4] + money * w[5])
        continuation = w[0] + money * (w[1] + money * w[2]) + annuity * slope
        gate = 1.0 / (1.0 + jnp.exp(-(exercise - continuation) / SMOOTHING))
        chance = flags[k] * gate
        discount = 1.0 / numeraire
        paid = exercise * discount
        values = values + NOTIONAL * survival * chance * paid
        kept.append(
            dict(
                numeraire=numeraire, survival=survival, annuity=annuity, floating=floating,
                inverse=inverse, money=money, slope=slope, gate=gate, chance=chance,
                discount=discount, paid=paid,
                d_money=w[1] + 2.0 * money * w[2] + annuity * (w[4] + 2.0 * money * w[5]),
            )
        )
        survival = survival * (1.0 - chance)
    value[...] = jnp.sum(values, axis=0, keepdims=True)

    one = jnp.ones((SHARDS, width), F32)
    zero = jnp.zeros((SHARDS, width), F32)
    s_mul, s_add, n_mul, n_add = one, zero, one, zero
    for k in reversed(range(PER)):
        e = kept[k]
        left = 1.0 - e["chance"]
        gain = scale * e["chance"] * e["paid"]
        s_mul, s_add = s_mul * left, s_add * left + gain
        e["n_push"] = -e["survival"] * gain * e["discount"]
        growth = growth_all[k]
        n_mul, n_add = n_mul * growth, (n_add + e["n_push"]) * growth
    survive_end = [None] * SHARDS
    numer_end = [None] * SHARDS
    s_now = jnp.zeros((1, width), F32)
    n_now = jnp.zeros((1, width), F32)
    for s in reversed(range(SHARDS)):
        survive_end[s] = s_now
        numer_end[s] = n_now
        s_now = s_mul[s : s + 1] * s_now + s_add[s : s + 1]
        n_now = n_mul[s : s + 1] * n_now + n_add[s : s + 1]
    d_survive = jnp.concatenate(survive_end, axis=0)
    d_numer = jnp.concatenate(numer_end, axis=0)
    for k in reversed(range(PER)):
        e = kept[k]
        d_numer = d_numer + e["n_push"]
        mult_numer[k] = d_numer * e["numeraire"]
        d_numer = d_numer * growth_all[k]
        d_chance = e["survival"] * (scale * e["paid"] - d_survive)
        d_score = d_chance * e["chance"] * (1.0 - e["gate"]) / SMOOTHING
        d_exercise = scale * e["survival"] * e["chance"] * e["discount"] + d_score
        d_money = -d_score * e["d_money"] / SMOOTHING
        ratio = d_money * e["inverse"]
        d_annuity = -d_score * e["slope"] - STRIKE * d_exercise - ratio * e["floating"] * e["inverse"]
        d_floating = d_exercise + ratio
        mult_tail[k] = -a * d_annuity
        mult_last[k] = d_floating * last_all[k]
        d_survive = d_survive * (1.0 - e["chance"]) + scale * e["chance"] * e["paid"]

    columns[...] = jnp.zeros((NF, 128), F32)
    pull = jnp.zeros((NF, width), F32)
    for s in reversed(range(SHARDS)):
        top = row_start(s)
        count = NF - top
        position = lax.broadcasted_iota(jnp.int32, (count, width), 0) + top
        lanes = lax.broadcasted_iota(jnp.int32, (count, 128), 1)
        if s < SHARDS - 1:
            below = row_start(s + 1)
            ratio = state[s, below:NF, :] / start[s + 1, below:NF, :]
            pull = zeros_above(below - top, pull[below - (NF - pull.shape[0]) :] * ratio)
        else:
            pull = pull[top:]

        def backward(step, pull):
            k = PER - 1 - step
            opening = 2 * (s * PER + k)
            h = 2.0 * a
            if s == 0:
                h = jnp.where(k == 0, a, 2.0 * a).astype(F32)
            sig = wide(sigma[s, k, top:NF, :])
            v = v_all[s, k, top:NF, :]
            later = v_all[s, k + 1, top:NF, :]
            push = mult_last[k, s : s + 1, :] + mult_tail[k, s : s + 1, :] * tail_all[s, k, top:NF, :]
            y = pull + jnp.where(position > opening, later * push, 0.0)
            high, low = halves(h * sig * y)
            high, low = zeros_above(top, high), zeros_above(top, low)
            rhs = jnp.concatenate([high, low, high], axis=0)
            du = jnp.dot(backward_lhs[top:NF, 0 : 3 * NF], rhs, preferred_element_type=F32)
            duv = du * v
            grown = v * mult_numer[k, s : s + 1, :]
            fixed = (position == opening) | (position == opening - 1)
            out = y + sig * duv * (1.0 - v) + jnp.where(fixed, grown, 0.0)
            by_vol = jnp.where(position > opening, y * w_all[s, k, top:NF, :] + duv, 0.0)
            summed = jnp.sum(by_vol, axis=1, keepdims=True)
            columns[top:NF, :] = jnp.where(lanes == s * PER + k, summed, columns[top:NF, :])
            return out

        pull = lax.fori_loop(0, PER, backward, pull)

    square[...] = jnp.zeros((128, 128), F32)
    square[0:NF, :] = columns[...]
    final = jnp.transpose(square[...])
    for s in range(SHARDS):
        vega[s] = final[s * PER : (s + 1) * PER, :]


def compute(path_weight, width, *arrays):
    inside = pl.BlockSpec(memory_space=pltpu.VMEM)
    big = pltpu.VMEM((SHARDS, PER, NF, width), F32)
    small = pltpu.VMEM((PER, SHARDS, width), F32)
    lhs = pltpu.VMEM((NF, 256), BF16)
    return pl.pallas_call(
        functools.partial(compute_kernel, path_weight),
        name="compute",
        out_shape=[
            jax.ShapeDtypeStruct((SHARDS, PER, 128), F32),
            jax.ShapeDtypeStruct((1, width), F32),
        ],
        in_specs=[inside] * len(arrays),
        out_specs=[inside] * 2,
        scratch_shapes=[
            pltpu.VMEM((128, 128), F32),
            pltpu.VMEM((256, 128), F32),
            lhs, lhs, lhs, lhs,
            pltpu.VMEM((SHARDS, PER, NF, 128), F32),
            pltpu.VMEM((NF, 128), F32),
            pltpu.VMEM((SHARDS, NF, width), F32),
            pltpu.VMEM((SHARDS, NF, width), F32),
            pltpu.VMEM((SHARDS, PER + 1, NF, width), F32),
            big, big,
            small, small, small, small,
            small, small, small,
            pltpu.VMEM((NF, 128), F32),
        ],
        compiler_params=pltpu.CompilerParams(vmem_limit_bytes=VMEM_LIMIT),
    )(*arrays)


def reduce_kernel(
    groups, width,
    part, value, vega, values,
    landed, values_landed, summed, spread,
    send_sem, recv_sem, value_send, value_recv, spread_send, spread_recv,
):
    me = lax.axis_index("tm")
    group = lax.axis_index("paths")
    barrier = pltpu.get_barrier_semaphore()
    for step in range(1, SHARDS):
        other = lax.rem(me + step, SHARDS)
        pl.semaphore_signal(barrier, inc=1, device_id={"tm": other}, device_id_type=MESH)
    for step in range(1, groups):
        other = lax.rem(group + step, groups)
        pl.semaphore_signal(barrier, inc=1, device_id={"paths": other}, device_id_type=MESH)
    pl.semaphore_wait(barrier, SHARDS - 1 + groups - 1)

    def block(step, source, target):
        return pltpu.make_async_remote_copy(
            src_ref=part.at[target], dst_ref=landed.at[source],
            send_sem=send_sem.at[step], recv_sem=recv_sem.at[source],
            device_id={"tm": target}, device_id_type=MESH,
        )

    def line(step, source, target):
        return pltpu.make_async_remote_copy(
            src_ref=value, dst_ref=values_landed.at[source],
            send_sem=value_send.at[step], recv_sem=value_recv.at[source],
            device_id={"tm": target}, device_id_type=MESH,
        )

    def share(step, source, target):
        return pltpu.make_async_remote_copy(
            src_ref=summed, dst_ref=spread.at[source],
            send_sem=spread_send.at[step], recv_sem=spread_recv.at[source],
            device_id={"paths": target}, device_id_type=MESH,
        )

    order = (4, 3, 5, 2, 6, 1, 7)
    for step in order:
        block(step, me, lax.rem(me + step, SHARDS)).start()
    for step in order:
        line(step, me, lax.rem(me + step, SHARDS)).start()
    landed[me] = part[me]
    values_landed[me] = value[...]
    for source in range(SHARDS):

        @pl.when(me != source)
        def _():
            block(0, source, source).wait_recv()

    total = landed[0]
    for source in range(1, SHARDS):
        total = total + landed[source]
    summed[...] = total
    spread[group] = total
    for source in range(SHARDS):

        @pl.when(me != source)
        def _():
            line(0, source, source).wait_recv()

    for step in range(1, groups):
        share(step, group, lax.rem(group + step, groups)).start()
    for source in range(SHARDS):
        values[0:1, source * width : (source + 1) * width] = values_landed[source]
    for step in order:
        block(step, me, lax.rem(me + step, SHARDS)).wait_send()
        line(step, me, lax.rem(me + step, SHARDS)).wait_send()
    for step in range(1, groups):
        share(step, group, lax.rem(group + step, groups)).wait_send()
    for step in range(1, groups):
        source = lax.rem(group + step, groups)
        share(0, source, source).wait_recv()
    total = spread[0]
    for source in range(1, groups):
        total = total + spread[source]
    vega[...] = total[:, 0:NF]


def reduce(groups, width, part, value):
    inside = pl.BlockSpec(memory_space=pltpu.VMEM)
    return pl.pallas_call(
        functools.partial(reduce_kernel, groups, width),
        name="reduce",
        out_shape=[
            jax.ShapeDtypeStruct((PER, NF), F32),
            jax.ShapeDtypeStruct((1, SHARDS * width), F32),
        ],
        in_specs=[inside] * 2,
        out_specs=[inside] * 2,
        scratch_shapes=[
            pltpu.VMEM((SHARDS, PER, 128), F32),
            pltpu.VMEM((SHARDS, 1, width), F32),
            pltpu.VMEM((PER, 128), F32),
            pltpu.VMEM((groups, PER, 128), F32),
            pltpu.SemaphoreType.DMA((SHARDS,)),
            pltpu.SemaphoreType.DMA((SHARDS,)),
            pltpu.SemaphoreType.DMA((SHARDS,)),
            pltpu.SemaphoreType.DMA((SHARDS,)),
            pltpu.SemaphoreType.DMA((groups,)),
            pltpu.SemaphoreType.DMA((groups,)),
        ],
        compiler_params=pltpu.CompilerParams(collective_id=1, has_side_effects=True),
    )(part, value)


def local(
    start_curve, loadings, vols, shocks, exercise_bits, regress, date_slot,
    ck_rates, ck_numer, ck_survive,
):
    groups = lax.axis_size("paths")
    path_count = shocks.shape[2]
    width = path_count // SHARDS
    path_weight = NOTIONAL / (path_count * groups)
    gathered = exchange(
        width, shocks, exercise_bits, ck_rates, ck_numer, ck_survive, vols, regress,
        date_slot.reshape(1, PER),
    )
    part, value = compute(
        path_weight, width, start_curve.reshape(1, NF), loadings, *gathered
    )
    vega, values = reduce(groups, width, part, value)
    return (vega, values.reshape(path_count))


def solution(mesh):
    return jax.shard_map(
        local,
        mesh=mesh,
        in_specs=(
            P(),
            P(),
            P("tm", None),
            P("tm", None, "paths"),
            P("tm", "paths"),
            P("tm", None),
            P("tm"),
            P("tm", None, "paths"),
            P("tm", "paths"),
            P("tm", "paths"),
        ),
        out_specs=(P("tm", None), P("paths")),
        check_vma=False,
    )
```

time: 465 us -> 70.5 us (0.15)
  matrix products: 198 us -> 0 us
  starting transfers between devices: 87.4 us -> 0 us
  waiting for transfers between devices: 81 us -> 0 us
  Pallas kernels: 0 us -> 67.8 us
  other arithmetic: 43 us -> 0 us
  blocking collectives: 33.4 us -> 0 us
  local copies, waits for them, and re-layouts: 9.65 us -> 1.88 us
  loops' own time: 6.87 us -> 0 us
    dot_general x451 -> x0, matrix products: 198 us -> none  [the longest x75 75.7 us: segment(): jnp.einsum('fi,fp->ip', factor_loads, shock_rows[offset_date], precision=...]
    ppermute x48 -> x0, starting transfers between devices: 69.4 us -> none  [passed_along(): lax.ppermute(value, axis, [(source, source + steps) for source in range(i...]
    ppermute x48 -> x0, waiting for transfers between devices: 68.8 us -> none  [passed_along(): lax.ppermute(value, axis, [(source, source + steps) for source in range(i...]
    pallas_call x0 -> x3, Pallas kernels: none -> 67.8 us  [the longest x1 27.2 us: exchange(): pl.pallas_call(functools.partial(exchange_kernel, width), name='exchange'...]
    all_to_all x1 -> x0, blocking collectives: 33.4 us -> none  [copy_for_each(): return lax.all_to_all(copies, axis, split_axis=0, concat_axis=0, tiled=True)]
    all_to_all x2 -> x0, starting transfers between devices: 18 us -> none  [copy_for_each(): return lax.all_to_all(copies, axis, split_axis=0, concat_axis=0, tiled=True)]
    all_to_all x2 -> x0, waiting for transfers between devices: 12.1 us -> none  [copy_for_each(): return lax.all_to_all(copies, axis, split_axis=0, concat_axis=0, tiled=True)]
    reduce_sum x78 -> x0, other arithmetic: 10.6 us -> none  [the longest x75 9.34 us: segment(): scaled = ACCRUAL * current * sigma[:, None] / (1.0 + ACCRUAL * current)]
  transfers between devices with their start and end apart: 50 -> 0, of which waited for: 17 -> 0; matrix products, arithmetic and copies ran while one was open for 3% -> 0% of each run, Pallas kernels for 0% -> 0%
where the time goes in v1:
time: 70.5 us; the launch traced here: 70.3 us
  Pallas kernels  67.8 us (96%)
  local copies, waits for them, and re-layouts  1.88 us (3%)
    pallas_call x1, Pallas kernels, exchange(): pl.pallas_call(functools.partial(exchange_kernel, width), name='exchange'...  27.2 us
    pallas_call x1, Pallas kernels, compute(): pl.pallas_call(functools.partial(compute_kernel, path_weight), name='comp...  21.9 us
    pallas_call x1, Pallas kernels, reduce(): pl.pallas_call(functools.partial(reduce_kernel, groups, width), name='red...  18.7 us
    unnamed x4, local copies, waits for them, and re-layouts  1.88 us

profile of v1, /device:TPU:1, one launch (start us, length us, event | category | flops | bytes accessed | tf_op | source)
XLA Modules:
  0.0 70.3 jit_solution(15427301456694166901)
XLA Ops:
  0.6 27.2 %exchange.1 = (f32[8,5,4,256]{3,2,1,0:T(4,128)}, s32[8,5,256]{2,1,0:T(8,128)}, f32[8,80,256]{2,1,0:T(8,128)}, f32[8,1,256]{2,1,0:T(1,128)}, f32[8,1,256]{2,1,0:T...) custom-call(f32[5,4,2048]{2,1,0:T(4,128)} %shocks.1, s32[5,2048]{1,0:T(8,128)} %bits.1, ...), custom_call_target="tpu_custom_call" | custom-call | tf_op jit(solution)/shard_map/exchange/pallas_call | solution.py:144
  27.8 21.9 %compute.1 = (f32[8,5,128]{2,1,0:T(8,128)}, f32[1,256]{1,0:T(1,128)}) custom-call(f32[1,80]{1,0:T(1,128)} %bitcast.4, f32[4,80]{1,0:T(4,128)} %loads.1, f32[8,5,4,256]{3,2,1,0:T(4,128)} %get-tuple-element.14.shocks, s32[8,5,256]{2,1,0:T(8,128)} %get-tuple-element.15.bits, f32[8,80,256]{2,1,0:T(8,128)} %get-tuple-element.16.rates, ...), custom_call_target="tpu_custom_call" | custom-call | tf_op jit(solution)/shard_map/compute/pallas_call | solution.py:445
  49.8 18.7 %reduce.1 = (f32[5,80]{1,0:T(8,128)}, f32[1,2048]{1,0:T(1,128)}) custom-call(f32[8,5,128]{2,1,0:T(8,128)} %get-tuple-element.22.part, f32[1,256]{1,0:T(1,128)} %get-tuple-element.23.value), custom_call_target="tpu_custom_call" | custom-call | tf_op jit(solution)/shard_map/reduce/pallas_call | solution.py:554
  68.4 0.0 copy-start
  68.4 1.3 %copy.14 = f32[5,80]{1,0:T(8,128)} copy(f32[5,80]{1,0:T(8,128)} %get-tuple-element.28) | data formatting | bytes 3200
  69.7 0.0 copy-done
  69.7 0.6 copy.15
Async XLA Ops:
  68.4 1.3 %copy-start = (f32[1,2048]{1,0:T(1,128)S(1)}, f32[1,2048]{1,0:T(1,128)}, u32[]{:S(2)}) copy-start(f32[1,2048]{1,0:T(1,128)} %get-tuple-element.25) | copy-start | bytes 24580

commit v2 on v0

v2 whole, which is shorter than its diff:
```python
import functools

import jax
import jax.numpy as jnp
from jax import lax
from jax.experimental import pallas as pl
from jax.experimental.pallas import tpu as pltpu
from jax.sharding import PartitionSpec as P

ACCRUAL = 0.25
STRIKE = 0.04
SMOOTHING = 0.01
NOTIONAL = 100.0
HIGHEST = lax.Precision.HIGHEST
MESH = pl.DeviceIdType.MESH
F32 = jnp.float32
BF16 = jnp.bfloat16

SHARDS = 8
PER = 5
NF = 80
VMEM_LIMIT = 60 * 1024 * 1024


def first_needed(shard):
    return max(2 * shard * PER - 1, 0)


def row_start(shard):
    return first_needed(shard) // 16 * 16


def sent_start(shard):
    return first_needed(shard) // 8 * 8

PHASES = (((0, 4, 5, 6, 7), (4, 5, 6, 7)), ((1, 2, 3), (0, 1, 2, 3)))
ORDER = (4, 3, 5, 2, 6, 1, 7)
KINDS = 8


def halves(x):
    high = x.astype(BF16)
    low = (x - high.astype(F32)).astype(BF16)
    return high, low


def split_f32(x):
    high = x.astype(BF16).astype(F32)
    return high, (x - high).astype(BF16).astype(F32)


def zeros_above(top, x):
    if top == 0:
        return x
    return jnp.concatenate([jnp.zeros((top, x.shape[1]), x.dtype), x], axis=0)


class Scratch:
    pass


def constants(c, loads, curve):
    lane = lax.broadcasted_iota(jnp.int32, (128, 128), 1)
    row = lax.broadcasted_iota(jnp.int32, (128, 128), 0)
    c.square[...] = jnp.zeros((128, 128), F32)
    raw = loads[...]
    c.square[0:4, 0:NF] = raw / jnp.sqrt(jnp.sum(raw * raw, axis=0, keepdims=True))
    padded = c.square[...]
    turned = jnp.transpose(padded)
    full = jnp.dot(turned, padded, precision=HIGHEST, preferred_element_type=F32)
    part_high, part_low = split_f32(padded)

    high, low = split_f32(jnp.where(row <= lane, full, 0.0))
    c.stack[...] = jnp.zeros((256, 128), F32)
    c.stack[0:NF, :] = high[:NF]
    c.stack[NF : 2 * NF, :] = high[:NF]
    c.stack[2 * NF : 3 * NF, :] = low[:NF]
    c.stack[240:244, :] = part_high[0:4]
    c.stack[244:248, :] = part_high[0:4]
    c.stack[248:252, :] = part_low[0:4]
    c.forward_lhs[...] = jnp.transpose(c.stack[...])[:NF].astype(BF16)

    high, low = split_f32(jnp.where(row >= lane, full, 0.0))
    c.stack[...] = jnp.zeros((256, 128), F32)
    c.stack[0:NF, :] = high[:NF]
    c.stack[NF : 2 * NF, :] = low[:NF]
    c.backward_lhs[...] = jnp.transpose(c.stack[...])[:NF].astype(BF16)

    lower = jnp.where((row <= lane) & (row < NF), 1.0, 0.0)
    c.stack[0:NF, :] = lower[:NF]
    c.stack[NF : 2 * NF, :] = lower[:NF]
    c.sums_lhs[...] = jnp.transpose(c.stack[...])[:NF].astype(BF16)
    upper = jnp.where((row >= lane) & (row < NF), 1.0, 0.0)
    c.stack[0:NF, :] = upper[:NF]
    c.stack[NF : 2 * NF, :] = upper[:NF]
    c.tails_lhs[...] = jnp.transpose(c.stack[...])[:NF].astype(BF16)

    c.square[...] = jnp.zeros((128, 128), F32)
    c.square[0:1, 0:NF] = curve[...]
    column = jnp.transpose(c.square[...])[:NF, 0:1]
    c.start[0][...] = jnp.broadcast_to(column, (NF, c.width))


def tables(c):
    lane = lax.broadcasted_iota(jnp.int32, (SHARDS, 128), 1)
    row = lax.broadcasted_iota(jnp.int32, (128, 128), 0)
    c.square[...] = jnp.zeros((128, 128), F32)
    for s in range(SHARDS):
        c.square[s * PER : (s + 1) * PER, 0:NF] = c.vols[s]
    turned = jnp.transpose(c.square[...])
    for s in range(SHARDS):
        top = row_start(s)
        for k in range(PER):
            d = s * PER + k
            column = jnp.broadcast_to(turned[top:NF, d : d + 1], (NF - top, 128))
            c.sigma[s, k, top:NF, :] = jnp.where(row[top:NF] >= 2 * d + 1, column, 0.0)
    c.square[...] = jnp.zeros((128, 128), F32)
    for s in range(SHARDS):
        c.square[s * PER : (s + 1) * PER, 0:6] = c.regress[s]
    ids = jnp.concatenate([c.slots[s] for s in range(SHARDS)], axis=0)
    hot = jnp.concatenate(
        [
            jnp.where(jnp.broadcast_to(ids[:, k : k + 1], (SHARDS, 128)) == lane, 1.0, 0.0)
            for k in range(PER)
        ],
        axis=0,
    )
    c.weights[...] = jnp.dot(hot, c.square[...], precision=HIGHEST, preferred_element_type=F32)


def flag_rows(c):
    for s in range(SHARDS):
        for k in range(PER):
            c.flags[k, s : s + 1, :] = c.bits[s, k : k + 1, :].astype(F32)


def forward_pass(c, shards):
    a, width = ACCRUAL, c.width

    def wide(x):
        return jnp.concatenate([x] * (width // 128), axis=1)

    for s in shards:
        top = row_start(s)
        if s > 0:
            position = lax.broadcasted_iota(jnp.int32, (NF - top, width), 0) + top
            c.start[s][top:NF, :] = jnp.where(
                position >= first_needed(s), c.rates[s - 1, top:NF, :], STRIKE
            )
        c.state[s][top:NF, :] = c.start[s][top:NF, :]

    def drift(s, k, held):
        top = row_start(s)
        if s == 0:
            h = jnp.where(k == 0, a, 2.0 * a).astype(F32)
            root = jnp.where(k == 0, a**0.5, (2.0 * a) ** 0.5).astype(F32)
        else:
            h, root = 2.0 * a, (2.0 * a) ** 0.5
        current = c.state[s][top:NF, :]
        opening = 2 * (s * PER + k)
        second = 1.0 + a * c.state[s][pl.ds(opening, 1), :]
        if s == 0:
            before = 1.0 + a * c.state[s][pl.ds(jnp.maximum(opening - 1, 0), 1), :]
            before = jnp.where(k == 0, 1.0, before)
        else:
            before = 1.0 + a * c.state[s][pl.ds(opening - 1, 1), :]
        c.growth[k, s : s + 1, :] = before * second
        scaled = a * current
        v = scaled / (1.0 + scaled)
        c.v[s][k, top:NF, :] = v
        sig = wide(c.sigma[s, k, top:NF, :])
        hsig = h * sig
        high, low = halves(hsig * v)
        shock = root * c.shocks[s, k]
        shock_high = shock.astype(BF16).astype(F32)
        noise = jnp.concatenate(
            [shock_high, shock - shock_high, shock_high, jnp.zeros_like(shock)], axis=0
        ).astype(BF16)
        high, low = zeros_above(top, high), zeros_above(top, low)
        rhs = jnp.concatenate([high, low, high, noise], axis=0)
        w = jnp.dot(c.forward_lhs[top:NF, :], rhs, preferred_element_type=F32)
        held[s] = (w, sig, hsig, current)

    def moved(s, k, held):
        top = row_start(s)
        w, sig, hsig, current = held[s]
        c.w[s][k, top:NF, :] = w - hsig
        current = current * jnp.exp(sig * (w - 0.5 * hsig))
        c.state[s][top:NF, :] = current
        position = lax.broadcasted_iota(jnp.int32, (NF - top, width), 0) + top
        living = position > 2 * (s * PER + k)
        logs = jnp.where(living, jnp.log(1.0 + a * current), 0.0)
        high, low = halves(logs)
        rhs = jnp.concatenate([zeros_above(top, high), zeros_above(top, low)], axis=0)
        total = jnp.dot(c.sums_lhs[top:NF, 0 : 2 * NF], rhs, preferred_element_type=F32)
        held[s] = (total, living)

    def bonds_of(s, k, held):
        top = row_start(s)
        total, living = held[s]
        bonds = jnp.where(living, jnp.exp(-total), 0.0)
        c.annuity[k, s : s + 1, :] = a * jnp.sum(bonds, axis=0, keepdims=True)
        c.last[k, s : s + 1, :] = bonds[NF - top - 1 : NF - top]
        high, low = halves(bonds)
        rhs = jnp.concatenate([zeros_above(top, high), zeros_above(top, low)], axis=0)
        c.tail[s][k, top:NF, :] = jnp.dot(
            c.tails_lhs[top:NF, 0 : 2 * NF], rhs, preferred_element_type=F32
        )

    def forward(k, carry):
        held = {}
        count = len(shards)
        for step in range(count + 2):
            if step >= 2:
                bonds_of(shards[step - 2], k, held)
            if 1 <= step <= count:
                moved(shards[step - 1], k, held)
            if step < count:
                drift(shards[step], k, held)
        return carry

    lax.fori_loop(0, PER, forward, 0)
    for s in shards:
        top = row_start(s)
        scaled = a * c.state[s][top:NF, :]
        c.v[s][PER, top:NF, :] = scaled / (1.0 + scaled)


def exercise_pass(c, shards, s_now, n_now):
    a, width = ACCRUAL, c.width
    low, count = shards[0], len(shards)
    rows = slice(low, low + count)

    def starts(ref):
        lines = [ref[s - 1] if s > 0 else jnp.ones((1, width), F32) for s in shards]
        return jnp.concatenate(lines, axis=0)

    numeraire, survival = starts(c.numer), starts(c.survive)
    scale = c.path_weight * NOTIONAL
    kept = []
    values = jnp.zeros((count, width), F32)
    for k in range(PER):
        growth = c.growth[k, rows, :]
        numeraire = numeraire * growth
        annuity = c.annuity[k, rows, :]
        last = c.last[k, rows, :]
        floating = 1.0 - last
        exercise = floating - STRIKE * annuity
        inverse = 1.0 / annuity
        money = (floating * inverse - STRIKE) / SMOOTHING
        w = [
            jnp.broadcast_to(
                c.weights[k * SHARDS + low : k * SHARDS + low + count, b : b + 1], (count, width)
            )
            for b in range(6)
        ]
        slope = w[3] + money * (w[4] + money * w[5])
        continuation = w[0] + money * (w[1] + money * w[2]) + annuity * slope
        gate = 1.0 / (1.0 + jnp.exp(-(exercise - continuation) / SMOOTHING))
        chance = c.flags[k, rows, :] * gate
        discount = 1.0 / numeraire
        paid = exercise * discount
        values = values + NOTIONAL * survival * chance * paid
        kept.append(
            dict(
                numeraire=numeraire, survival=survival, floating=floating, growth=growth,
                last=last, inverse=inverse, slope=slope, gate=gate, chance=chance,
                discount=discount, paid=paid,
                d_money=w[1] + 2.0 * money * w[2] + annuity * (w[4] + 2.0 * money * w[5]),
            )
        )
        survival = survival * (1.0 - chance)

    one, zero = jnp.ones((count, width), F32), jnp.zeros((count, width), F32)
    s_mul, s_add, n_mul, n_add = one, zero, one, zero
    for k in reversed(range(PER)):
        e = kept[k]
        left = 1.0 - e["chance"]
        gain = scale * e["chance"] * e["paid"]
        s_mul, s_add = s_mul * left, s_add * left + gain
        e["n_push"] = -e["survival"] * gain * e["discount"]
        n_mul, n_add = n_mul * e["growth"], (n_add + e["n_push"]) * e["growth"]
    survive_end, numer_end = [None] * count, [None] * count
    for i in reversed(range(count)):
        survive_end[i], numer_end[i] = s_now, n_now
        s_now = s_mul[i : i + 1] * s_now + s_add[i : i + 1]
        n_now = n_mul[i : i + 1] * n_now + n_add[i : i + 1]
    d_survive = jnp.concatenate(survive_end, axis=0)
    d_numer = jnp.concatenate(numer_end, axis=0)
    for k in reversed(range(PER)):
        e = kept[k]
        d_numer = d_numer + e["n_push"]
        c.mult_numer[k, rows, :] = d_numer * e["numeraire"]
        d_numer = d_numer * e["growth"]
        d_chance = e["survival"] * (scale * e["paid"] - d_survive)
        d_score = d_chance * e["chance"] * (1.0 - e["gate"]) / SMOOTHING
        d_exercise = scale * e["survival"] * e["chance"] * e["discount"] + d_score
        d_money = -d_score * e["d_money"] / SMOOTHING
        ratio = d_money * e["inverse"]
        d_annuity = -d_score * e["slope"] - STRIKE * d_exercise - ratio * e["floating"] * e["inverse"]
        d_floating = d_exercise + ratio
        c.mult_tail[k, rows, :] = -a * d_annuity
        c.mult_last[k, rows, :] = d_floating * e["last"]
        d_survive = d_survive * (1.0 - e["chance"]) + scale * e["chance"] * e["paid"]
    return s_now, n_now, jnp.sum(values, axis=0, keepdims=True)


def backward_shard(c, s, pull):
    a, width = ACCRUAL, c.width
    top = row_start(s)
    count = NF - top
    position = lax.broadcasted_iota(jnp.int32, (count, width), 0) + top
    if s < SHARDS - 1:
        below = row_start(s + 1)
        ratio = c.state[s][below:NF, :] / c.start[s + 1][below:NF, :]
        pull = zeros_above(below - top, pull * ratio)

    def backward(step, pull):
        k = PER - 1 - step
        opening = 2 * (s * PER + k)
        h = 2.0 * a
        if s == 0:
            h = jnp.where(k == 0, a, 2.0 * a).astype(F32)
        narrow = c.sigma[s, k, top:NF, :]
        sig = jnp.concatenate([narrow] * (width // 128), axis=1)
        v = c.v[s][k, top:NF, :]
        push = c.mult_last[k, s : s + 1, :] + c.mult_tail[k, s : s + 1, :] * c.tail[s][k, top:NF, :]
        y = pull + jnp.where(position > opening, c.v[s][k + 1, top:NF, :] * push, 0.0)
        part = zeros_above(top, (h * sig * y).astype(BF16))
        rhs = jnp.concatenate([part, part], axis=0)
        du = jnp.dot(c.backward_lhs[top:NF, 0 : 2 * NF], rhs, preferred_element_type=F32)
        fixed = (position == opening) | (position == opening - 1)
        base = y + jnp.where(fixed, v * c.mult_numer[k, s : s + 1, :], 0.0)
        factor = sig * (v * (1.0 - v))
        out = base + factor * du
        by_vol = jnp.where(position > opening, y * c.w[s][k, top:NF, :] + du * v, 0.0)
        folded = by_vol[:, 0:128]
        for piece in range(1, width // 128):
            folded = folded + by_vol[:, piece * 128 : (piece + 1) * 128]
        c.by_vol[s][k, top:NF, :] = folded
        return out

    return lax.fori_loop(0, PER, backward, pull, unroll=UNROLL)


def sum_paths(c, shards):
    for s in shards:
        top = row_start(s)
        lanes = lax.broadcasted_iota(jnp.int32, (NF - top, 128), 1)
        gathered = c.square[top:NF, :]
        for k in range(PER):
            summed = jnp.sum(c.by_vol[s][k, top:NF, :], axis=1, keepdims=True)
            gathered = jnp.where(lanes == s * PER + k, summed, gathered)
        c.square[top:NF, :] = gathered


UNROLL = True


def kernel(
    path_weight, groups,
    curve, loads, shocks, bits, rates, numer, survive, vols, regress, slots,
    vega, values,
    shocks_x, bits_x, rates_x, numer_x, survive_x, vols_x, regress_x, slots_x,
    square, stack, forward_lhs, backward_lhs, sums_lhs, tails_lhs, sigma, weights,
    growth, annuity, last, flags, mult_tail, mult_last, mult_numer,
    part, landed, value, values_landed, summed, spread,
    *rest,
):
    per_shard, sems = rest[: 7 * SHARDS], rest[7 * SHARDS :]
    (send_sem, recv_sem, local_sem, part_send, part_recv, value_send, value_recv,
     spread_send, spread_recv) = sems
    c = Scratch()
    c.path_weight, c.width = path_weight, shocks_x.shape[3]
    c.shocks, c.bits, c.rates, c.numer, c.survive = shocks_x, bits_x, rates_x, numer_x, survive_x
    c.vols, c.regress, c.slots = vols_x, regress_x, slots_x
    c.square, c.stack, c.sigma, c.weights = square, stack, sigma, weights
    c.forward_lhs, c.backward_lhs = forward_lhs, backward_lhs
    c.sums_lhs, c.tails_lhs = sums_lhs, tails_lhs
    c.growth, c.annuity, c.last, c.flags = growth, annuity, last, flags
    c.mult_tail, c.mult_last, c.mult_numer = mult_tail, mult_last, mult_numer
    c.state, c.start, c.v, c.w, c.tail, c.by_vol, _ = (
        per_shard[i * SHARDS : (i + 1) * SHARDS] for i in range(7)
    )
    width = c.width
    me = lax.axis_index("tm")
    group = lax.axis_index("paths")

    barrier = pltpu.get_barrier_semaphore()
    for step in ORDER:
        other = lax.rem(me + step, SHARDS)
        pl.semaphore_signal(barrier, inc=1, device_id={"tm": other}, device_id_type=MESH)
    for step in range(1, groups):
        other = lax.rem(group + step, groups)
        pl.semaphore_signal(barrier, inc=1, device_id={"paths": other}, device_id_type=MESH)

    def cut(target):
        return pl.ds(pl.multiple_of(target * width, width), width)

    def pair_of(kind, source, target):
        if kind == 0:
            return vols, vols_x.at[source]
        if kind == 1:
            return regress, regress_x.at[source]
        if kind == 2:
            return slots, slots_x.at[source]
        if kind == 3:
            return shocks.at[:, :, cut(target)], shocks_x.at[source]
        if kind == 4:
            return bits.at[:, cut(target)], bits_x.at[source]
        if kind == 5:
            return numer.at[:, cut(target)], numer_x.at[source]
        if kind == 6:
            return survive.at[:, cut(target)], survive_x.at[source]
        top = sent_start(source + 1)
        rows = pl.ds(top, NF - top)
        return rates.at[0, rows, cut(target)], rates_x.at[source, rows, :]

    def here(kind, source):
        src, dst = pair_of(kind, source, source)
        return pltpu.make_async_copy(src, dst, local_sem.at[kind])

    def remote(kind, source, step, target):
        src, dst = pair_of(kind, source, target)
        return pltpu.make_async_remote_copy(
            src_ref=src, dst_ref=dst,
            send_sem=send_sem.at[kind, step], recv_sem=recv_sem.at[kind, source],
            device_id={"tm": target}, device_id_type=MESH,
        )

    def rates_by_source(action):
        for source in range(SHARDS - 1):

            @pl.when(me == source)
            def _():
                action(source)

    def start_rates(source):
        for step in ORDER:
            remote(7, source, step, lax.rem(me + step, SHARDS)).start()

    def end_rates(source):
        for step in ORDER:
            remote(7, source, step, lax.rem(me + step, SHARDS)).wait_send()

    def await_kinds(kinds, sources):
        for source in sources:

            @pl.when(me != source)
            def _():
                for kind in kinds:
                    remote(kind, source, 0, source).wait_recv()

            @pl.when(me == source)
            def _():
                for kind in kinds:
                    here(kind, source).wait()

    for kind in range(7):
        here(kind, me).start()
    rates_by_source(lambda source: here(7, source).start())
    constants(c, loads, curve)
    pl.semaphore_wait(barrier, SHARDS - 1 + groups - 1)
    for kinds in ((0, 1, 2), (3, 4, 5, 6)):
        for step in ORDER:
            for kind in kinds:
                remote(kind, me, step, lax.rem(me + step, SHARDS)).start()
    rates_by_source(start_rates)

    everyone = range(SHARDS)
    await_kinds((0, 1, 2), everyone)
    tables(c)
    await_kinds((3, 4, 5, 6), everyone)
    flag_rows(c)

    s_now = jnp.zeros((1, width), F32)
    n_now = jnp.zeros((1, width), F32)
    pull = jnp.zeros((NF - row_start(SHARDS - 1), width), F32)
    paid = None
    square[...] = jnp.zeros((128, 128), F32)
    for first_shards, shards in PHASES:
        await_kinds((7,), [s - 1 for s in reversed(first_shards) if s > 0])
        forward_pass(c, first_shards)
        s_now, n_now, gains = exercise_pass(c, shards, s_now, n_now)
        paid = gains if paid is None else paid + gains
        if shards[0] == 0:
            value[...] = paid
        for s in reversed(shards):
            pull = backward_shard(c, s, pull)
        sum_paths(c, shards)

    turned = jnp.transpose(square[...])
    for s in range(SHARDS):
        part[s] = turned[s * PER : (s + 1) * PER, :]

    def block(step, source, target):
        return pltpu.make_async_remote_copy(
            src_ref=part.at[target], dst_ref=landed.at[source],
            send_sem=part_send.at[step], recv_sem=part_recv.at[source],
            device_id={"tm": target}, device_id_type=MESH,
        )

    def line(step, source, target):
        return pltpu.make_async_remote_copy(
            src_ref=value, dst_ref=values_landed.at[source],
            send_sem=value_send.at[step], recv_sem=value_recv.at[source],
            device_id={"tm": target}, device_id_type=MESH,
        )

    def share(step, source, target):
        return pltpu.make_async_remote_copy(
            src_ref=summed, dst_ref=spread.at[source],
            send_sem=spread_send.at[step], recv_sem=spread_recv.at[source],
            device_id={"paths": target}, device_id_type=MESH,
        )

    for step in ORDER:
        line(step, me, lax.rem(me + step, SHARDS)).start()
    for step in ORDER:
        block(step, me, lax.rem(me + step, SHARDS)).start()
    landed[me] = part[me]
    values_landed[me] = value[...]
    for kind in range(7):
        for step in ORDER:
            remote(kind, me, step, lax.rem(me + step, SHARDS)).wait_send()
    rates_by_source(end_rates)
    for source in everyone:

        @pl.when(me != source)
        def _():
            block(0, source, source).wait_recv()

    total = landed[0]
    for source in range(1, SHARDS):
        total = total + landed[source]
    summed[...] = total
    spread[group] = total
    for source in everyone:

        @pl.when(me != source)
        def _():
            line(0, source, source).wait_recv()

    for step in range(1, groups):
        share(step, group, lax.rem(group + step, groups)).start()
    for source in everyone:
        values[0:1, source * width : (source + 1) * width] = values_landed[source]
    for step in ORDER:
        block(step, me, lax.rem(me + step, SHARDS)).wait_send()
        line(step, me, lax.rem(me + step, SHARDS)).wait_send()
    for step in range(1, groups):
        share(step, group, lax.rem(group + step, groups)).wait_send()
    for step in range(1, groups):
        source = lax.rem(group + step, groups)
        share(0, source, source).wait_recv()
    total = spread[0]
    for source in range(1, groups):
        total = total + spread[source]
    vega[...] = total[:, 0:NF]


def local(
    start_curve, loadings, vols, shocks, exercise_bits, regress, date_slot,
    ck_rates, ck_numer, ck_survive,
):
    groups = lax.axis_size("paths")
    path_count = shocks.shape[2]
    width = path_count // SHARDS
    inside = pl.BlockSpec(memory_space=pltpu.VMEM)
    anywhere = pl.BlockSpec(memory_space=pl.ANY)
    small = pltpu.VMEM((PER, SHARDS, width), F32)
    lhs = pltpu.VMEM((NF, 256), BF16)
    plane = pltpu.VMEM((NF, width), F32)
    dates = pltpu.VMEM((PER, NF, width), F32)
    dma = pltpu.SemaphoreType.DMA
    vega, values = pl.pallas_call(
        functools.partial(kernel, NOTIONAL / (path_count * groups), groups),
        name="pathwise_vega",
        out_shape=[
            jax.ShapeDtypeStruct((PER, NF), F32),
            jax.ShapeDtypeStruct((1, path_count), F32),
        ],
        in_specs=[inside] * 2 + [anywhere] * 8,
        out_specs=[inside] * 2,
        scratch_shapes=[
            pltpu.VMEM((SHARDS, PER, 4, width), F32),
            pltpu.VMEM((SHARDS, PER, width), jnp.int32),
            pltpu.VMEM((SHARDS, NF, width), F32),
            pltpu.VMEM((SHARDS, 1, width), F32),
            pltpu.VMEM((SHARDS, 1, width), F32),
            pltpu.VMEM((SHARDS, PER, NF), F32),
            pltpu.VMEM((SHARDS, PER, 6), F32),
            pltpu.VMEM((SHARDS, 1, PER), jnp.int32),
            pltpu.VMEM((128, 128), F32),
            pltpu.VMEM((256, 128), F32),
            lhs, lhs, lhs, lhs,
            pltpu.VMEM((SHARDS, PER, NF, 128), F32),
            pltpu.VMEM((PER * SHARDS, 128), F32),
            small, small, small, small,
            small, small, small,
            pltpu.VMEM((SHARDS, PER, 128), F32),
            pltpu.VMEM((SHARDS, PER, 128), F32),
            pltpu.VMEM((1, width), F32),
            pltpu.VMEM((SHARDS, 1, width), F32),
            pltpu.VMEM((PER, 128), F32),
            pltpu.VMEM((groups, PER, 128), F32),
        ]
        + [plane] * SHARDS
        + [plane] * SHARDS
        + [pltpu.VMEM((PER + 1, NF, width), F32)] * SHARDS
        + [dates] * SHARDS
        + [dates] * SHARDS
        + [pltpu.VMEM((PER, NF, 128), F32)] * SHARDS
        + [pltpu.VMEM((8, 128), F32)] * SHARDS
        + [
            dma((KINDS, SHARDS)), dma((KINDS, SHARDS)), dma((KINDS,)),
            dma((SHARDS,)), dma((SHARDS,)), dma((SHARDS,)), dma((SHARDS,)),
            dma((groups,)), dma((groups,)),
        ],
        compiler_params=pltpu.CompilerParams(
            collective_id=0, has_side_effects=True, vmem_limit_bytes=VMEM_LIMIT
        ),
    )(
        start_curve.reshape(1, NF), loadings, shocks, exercise_bits, ck_rates, ck_numer,
        ck_survive, vols, regress, date_slot.reshape(1, PER),
    )
    return (vega, values.reshape(path_count))


def solution(mesh):
    return jax.shard_map(
        local,
        mesh=mesh,
        in_specs=(
            P(),
            P(),
            P("tm", None),
            P("tm", None, "paths"),
            P("tm", "paths"),
            P("tm", None),
            P("tm"),
            P("tm", None, "paths"),
            P("tm", "paths"),
            P("tm", "paths"),
        ),
        out_specs=(P("tm", None), P("paths")),
        check_vma=False,
    )
```

time: 465 us -> 58.9 us (0.13)
  matrix products: 198 us -> 0 us
  starting transfers between devices: 87.4 us -> 0 us
  waiting for transfers between devices: 81 us -> 0 us
  Pallas kernels: 0 us -> 56.2 us
  other arithmetic: 43 us -> 0 us
  blocking collectives: 33.4 us -> 0 us
  local copies, waits for them, and re-layouts: 9.65 us -> 1.88 us
  loops' own time: 6.87 us -> 0 us
    dot_general x451 -> x0, matrix products: 198 us -> none  [the longest x75 75.7 us: segment(): jnp.einsum('fi,fp->ip', factor_loads, shock_rows[offset_date], precision=...]
    ppermute x48 -> x0, starting transfers between devices: 69.4 us -> none  [passed_along(): lax.ppermute(value, axis, [(source, source + steps) for source in range(i...]
    ppermute x48 -> x0, waiting for transfers between devices: 68.8 us -> none  [passed_along(): lax.ppermute(value, axis, [(source, source + steps) for source in range(i...]
    pallas_call x0 -> x1, Pallas kernels: none -> 56.2 us  [local(): pl.pallas_call(functools.partial(kernel, NOTIONAL / (path_count * groups)...]
    all_to_all x1 -> x0, blocking collectives: 33.4 us -> none  [copy_for_each(): return lax.all_to_all(copies, axis, split_axis=0, concat_axis=0, tiled=True)]
    all_to_all x2 -> x0, starting transfers between devices: 18 us -> none  [copy_for_each(): return lax.all_to_all(copies, axis, split_axis=0, concat_axis=0, tiled=True)]
    all_to_all x2 -> x0, waiting for transfers between devices: 12.1 us -> none  [copy_for_each(): return lax.all_to_all(copies, axis, split_axis=0, concat_axis=0, tiled=True)]
    reduce_sum x78 -> x0, other arithmetic: 10.6 us -> none  [the longest x75 9.34 us: segment(): scaled = ACCRUAL * current * sigma[:, None] / (1.0 + ACCRUAL * current)]
  transfers between devices with their start and end apart: 50 -> 0, of which waited for: 17 -> 0; matrix products, arithmetic and copies ran while one was open for 3% -> 0% of each run, Pallas kernels for 0% -> 0%
where the time goes in v2:
time: 58.9 us; the launch traced here: 58.8 us
  Pallas kernels  56.2 us (95%)
  local copies, waits for them, and re-layouts  1.88 us (3%)
  between operations  0.65 us (1%)
    pallas_call x1, Pallas kernels, local(): pl.pallas_call(functools.partial(kernel, NOTIONAL / (path_count * groups)...  56.2 us
    unnamed x4, local copies, waits for them, and re-layouts  1.88 us

profile of v2, /device:TPU:1, one launch (start us, length us, event | category | flops | bytes accessed | tf_op | source)
XLA Modules:
  0.0 58.8 jit_solution(15306834988389165982)
XLA Ops:
  0.6 56.2 %pathwise_vega.1 = (f32[5,80]{1,0:T(8,128)}, f32[1,2048]{1,0:T(1,128)}) custom-call(f32[1,80]{1,0:T(1,128)} %bitcast.4, f32[4,80]{1,0:T(4,128)} %loads.1, f32[5,4,2048]{2,1,0:T(4,128)} %shocks.1, s32[5,2048]{1,0:T(8,128)} %bits.1, f32[1,80,2048]{2,1,0:T(8,128)} %rates.1, f32[1,2048]{1,0:T(1,128)} %numer.1, f32[1,2048]{1,0:T(1,128)} %survive.1, ...), custom_call_target="tpu_custom_call" | custom-call | tf_op jit(solution)/shard_map/pathwise_vega/pallas_call | solution.py:576
  56.9 0.0 copy-start
  56.9 1.3 %copy.14 = f32[5,80]{1,0:T(8,128)} copy(f32[5,80]{1,0:T(8,128)} %get-tuple-element.8) | data formatting | bytes 3200
  58.2 0.0 copy-done
  58.2 0.6 %copy.15 = f32[2048]{0:T(1024)} copy(f32[2048]{0:T(1024)S(1)} %bitcast.3) | data formatting | bytes 16384
Async XLA Ops:
  56.9 1.3 %copy-start = (f32[1,2048]{1,0:T(1,128)S(1)}, f32[1,2048]{1,0:T(1,128)}, u32[]{:S(2)}) copy-start(f32[1,2048]{1,0:T(1,128)} %get-tuple-element.5) | copy-start | bytes 24580

commit v3 on v2

--- a/solution.py
+++ b/solution.py
@@ -36,6 +36,9 @@
 PHASES = (((0, 4, 5, 6, 7), (4, 5, 6, 7)), ((1, 2, 3), (0, 1, 2, 3)))
 ORDER = (4, 3, 5, 2, 6, 1, 7)
 KINDS = 8
+EARLY = {0: (3, 4), 1: (), 2: (), 3: (5, 6, 7), 4: (5, 6, 7, 3, 4), 5: (5, 6, 7, 3, 4), 6: (5, 6, 7, 3, 4), 7: (3, 4)}
+LATE = {0: (5, 6, 7), 1: (3, 4, 5, 6, 7), 2: (3, 4, 5, 6, 7), 3: (3, 4), 4: (), 5: (), 6: (), 7: ()}
+GATE = ()
 
 
 def halves(x):
@@ -128,8 +131,8 @@
     c.weights[...] = jnp.dot(hot, c.square[...], precision=HIGHEST, preferred_element_type=F32)
 
 
-def flag_rows(c):
-    for s in range(SHARDS):
+def flag_rows(c, shards):
+    for s in shards:
         for k in range(PER):
             c.flags[k, s : s + 1, :] = c.bits[s, k : k + 1, :].astype(F32)
 
@@ -219,7 +222,7 @@
                 drift(shards[step], k, held)
         return carry
 
-    lax.fori_loop(0, PER, forward, 0)
+    lax.fori_loop(0, PER, forward, 0, unroll=True)
     for s in shards:
         top = row_start(s)
         scaled = a * c.state[s][top:NF, :]
@@ -340,7 +343,7 @@
         c.by_vol[s][k, top:NF, :] = folded
         return out
 
-    return lax.fori_loop(0, PER, backward, pull, unroll=UNROLL)
+    return lax.fori_loop(0, PER, backward, pull, unroll=True)
 
 
 def sum_paths(c, shards):
@@ -352,9 +355,6 @@
             summed = jnp.sum(c.by_vol[s][k, top:NF, :], axis=1, keepdims=True)
             gathered = jnp.where(lanes == s * PER + k, summed, gathered)
         c.square[top:NF, :] = gathered
-
-
-UNROLL = True
 
 
 def kernel(
@@ -367,7 +367,7 @@
     part, landed, value, values_landed, summed, spread,
     *rest,
 ):
-    per_shard, sems = rest[: 7 * SHARDS], rest[7 * SHARDS :]
+    per_shard, sems = rest[: 6 * SHARDS], rest[6 * SHARDS :]
     (send_sem, recv_sem, local_sem, part_send, part_recv, value_send, value_recv,
      spread_send, spread_recv) = sems
     c = Scratch()
@@ -379,8 +379,8 @@
     c.sums_lhs, c.tails_lhs = sums_lhs, tails_lhs
     c.growth, c.annuity, c.last, c.flags = growth, annuity, last, flags
     c.mult_tail, c.mult_last, c.mult_numer = mult_tail, mult_last, mult_numer
-    c.state, c.start, c.v, c.w, c.tail, c.by_vol, _ = (
-        per_shard[i * SHARDS : (i + 1) * SHARDS] for i in range(7)
+    c.state, c.start, c.v, c.w, c.tail, c.by_vol = (
+        per_shard[i * SHARDS : (i + 1) * SHARDS] for i in range(6)
     )
     width = c.width
     me = lax.axis_index("tm")
@@ -428,58 +428,73 @@
             device_id={"tm": target}, device_id_type=MESH,
         )
 
-    def rates_by_source(action):
-        for source in range(SHARDS - 1):
+    def by_source(plan, action):
+        for source in everyone:
+            if plan[source]:
+
+                @pl.when(me == source)
+                def _():
+                    action(source, plan[source])
+
+    def start_sends(source, kinds):
+        for step in ORDER:
+            for kind in kinds:
+                remote(kind, source, step, lax.rem(me + step, SHARDS)).start()
+
+    def end_sends(source, kinds):
+        for step in ORDER:
+            for kind in kinds:
+                remote(kind, source, step, lax.rem(me + step, SHARDS)).wait_send()
+
+    def start_here(source, kinds):
+        for kind in kinds:
+            here(kind, source).start()
+
+    def await_kinds(kinds, sources):
+        for source in sources:
+            wanted = [kind for kind in kinds if (kind, source) not in seen]
+            seen.update((kind, source) for kind in wanted)
+            if not wanted:
+                continue
+
+            @pl.when(me != source)
+            def _():
+                for kind in wanted:
+                    remote(kind, source, 0, source).wait_recv()
 
             @pl.when(me == source)
             def _():
-                action(source)
-
-    def start_rates(source):
-        for step in ORDER:
-            remote(7, source, step, lax.rem(me + step, SHARDS)).start()
-
-    def end_rates(source):
-        for step in ORDER:
-            remote(7, source, step, lax.rem(me + step, SHARDS)).wait_send()
-
-    def await_kinds(kinds, sources):
-        for source in sources:
-
-            @pl.when(me != source)
-            def _():
-                for kind in kinds:
-                    remote(kind, source, 0, source).wait_recv()
-
-            @pl.when(me == source)
-            def _():
-                for kind in kinds:
+                for kind in wanted:
                     here(kind, source).wait()
 
-    for kind in range(7):
+    everyone = range(SHARDS)
+    seen = set()
+    for kind in range(3):
         here(kind, me).start()
-    rates_by_source(lambda source: here(7, source).start())
+    by_source(EARLY, start_here)
+    by_source(LATE, start_here)
     constants(c, loads, curve)
     pl.semaphore_wait(barrier, SHARDS - 1 + groups - 1)
-    for kinds in ((0, 1, 2), (3, 4, 5, 6)):
-        for step in ORDER:
-            for kind in kinds:
-                remote(kind, me, step, lax.rem(me + step, SHARDS)).start()
-    rates_by_source(start_rates)
-
-    everyone = range(SHARDS)
+    start_sends(me, (0, 1, 2))
+    by_source(EARLY, start_sends)
     await_kinds((0, 1, 2), everyone)
+    for kinds, source in GATE:
+        await_kinds(kinds, (source,))
+    by_source(LATE, start_sends)
     tables(c)
-    await_kinds((3, 4, 5, 6), everyone)
-    flag_rows(c)
 
     s_now = jnp.zeros((1, width), F32)
     n_now = jnp.zeros((1, width), F32)
     pull = jnp.zeros((NF - row_start(SHARDS - 1), width), F32)
     paid = None
+    flagged = set()
     square[...] = jnp.zeros((128, 128), F32)
     for first_shards, shards in PHASES:
-        await_kinds((7,), [s - 1 for s in reversed(first_shards) if s > 0])
+        fresh = [s for s in dict.fromkeys(first_shards + shards) if s not in flagged]
+        flagged.update(fresh)
+        await_kinds((3, 4), fresh)
+        flag_rows(c, fresh)
+        await_kinds((5, 6, 7), [s - 1 for s in reversed(fresh) if s > 0])
         forward_pass(c, first_shards)
         s_now, n_now, gains = exercise_pass(c, shards, s_now, n_now)
         paid = gains if paid is None else paid + gains
@@ -520,10 +535,9 @@
         block(step, me, lax.rem(me + step, SHARDS)).start()
     landed[me] = part[me]
     values_landed[me] = value[...]
-    for kind in range(7):
-        for step in ORDER:
-            remote(kind, me, step, lax.rem(me + step, SHARDS)).wait_send()
-    rates_by_source(end_rates)
+    end_sends(me, (0, 1, 2))
+    by_source(EARLY, end_sends)
+    by_source(LATE, end_sends)
     for source in everyone:
 
         @pl.when(me != source)
@@ -611,7 +625,6 @@
         + [dates] * SHARDS
         + [dates] * SHARDS
         + [pltpu.VMEM((PER, NF, 128), F32)] * SHARDS
-        + [pltpu.VMEM((8, 128), F32)] * SHARDS
         + [
             dma((KINDS, SHARDS)), dma((KINDS, SHARDS)), dma((KINDS,)),
             dma((SHARDS,)), dma((SHARDS,)), dma((SHARDS,)), dma((SHARDS,)),

time: 58.9 us -> 52.8 us (0.90)
  Pallas kernels: 56.2 us -> 50.2 us
    pallas_call x1, Pallas kernels: 56.2 us -> 50.2 us  [local(): pl.pallas_call(functools.partial(kernel, NOTIONAL / (path_count * groups)...]
where the time goes in v3:
time: 52.8 us; the launch traced here: 52.7 us
  Pallas kernels  50.2 us (95%)
  local copies, waits for them, and re-layouts  1.88 us (4%)
  between operations  0.65 us (1%)
    pallas_call x1, Pallas kernels, local(): pl.pallas_call(functools.partial(kernel, NOTIONAL / (path_count * groups)...  50.2 us
    unnamed x4, local copies, waits for them, and re-layouts  1.88 us

profile of v3, /device:TPU:1, one launch (start us, length us, event | category | flops | bytes accessed | tf_op | source)
XLA Modules:
  0.0 52.7 jit_solution(5139512359844556415)
XLA Ops:
  0.6 50.2 %pathwise_vega.1 = (f32[5,80]{1,0:T(8,128)}, f32[1,2048]{1,0:T(1,128)}) custom-call(f32[1,80]{1,0:T(1,128)} %bitcast.4, f32[4,80]{1,0:T(4,128)} %loads.1, f32[5,4,2048]{2,1,0:T(4,128)} %shocks.1, s32[5,2048]{1,0:T(8,128)} %bits.1, f32[1,80,2048]{2,1,0:T(8,128)} %rates.1, f32[1,2048]{1,0:T(1,128)} %numer.1, f32[1,2048]{1,0:T(1,128)} %survive.1, ...), custom_call_target="tpu_custom_call" | custom-call | tf_op jit(solution)/shard_map/pathwise_vega/pallas_call | solution.py:590
  50.8 0.0 copy-start
  50.8 1.3 %copy.14 = f32[5,80]{1,0:T(8,128)} copy(f32[5,80]{1,0:T(8,128)} %get-tuple-element.8) | data formatting | bytes 3200
  52.1 0.0 copy-done
  52.1 0.6 %copy.15 = f32[2048]{0:T(1024)} copy(f32[2048]{0:T(1024)S(1)} %bitcast.3) | data formatting | bytes 16384
Async XLA Ops:
  50.8 1.3 %copy-start = (f32[1,2048]{1,0:T(1,128)S(1)}, f32[1,2048]{1,0:T(1,128)}, u32[]{:S(2)}) copy-start(f32[1,2048]{1,0:T(1,128)} %get-tuple-element.5) | copy-start | bytes 24580

commit v4 on v3

--- a/solution.py
+++ b/solution.py
@@ -38,7 +38,6 @@
 KINDS = 8
 EARLY = {0: (3, 4), 1: (), 2: (), 3: (5, 6, 7), 4: (5, 6, 7, 3, 4), 5: (5, 6, 7, 3, 4), 6: (5, 6, 7, 3, 4), 7: (3, 4)}
 LATE = {0: (5, 6, 7), 1: (3, 4, 5, 6, 7), 2: (3, 4, 5, 6, 7), 3: (3, 4), 4: (), 5: (), 6: (), 7: ()}
-GATE = ()
 
 
 def halves(x):
@@ -359,8 +358,9 @@
 
 def kernel(
     path_weight, groups,
-    curve, loads, shocks, bits, rates, numer, survive, vols, regress, slots,
+    curve_in, loads_in, shocks, bits, rates, numer, survive, vols, regress, slots,
     vega, values,
+    curve, loads,
     shocks_x, bits_x, rates_x, numer_x, survive_x, vols_x, regress_x, slots_x,
     square, stack, forward_lhs, backward_lhs, sums_lhs, tails_lhs, sigma, weights,
     growth, annuity, last, flags, mult_tail, mult_last, mult_numer,
@@ -469,19 +469,25 @@
 
     everyone = range(SHARDS)
     seen = set()
+    copies = [
+        pltpu.make_async_copy(source, target, local_sem.at[KINDS + i])
+        for i, (source, target) in enumerate(((curve_in, curve), (loads_in, loads)))
+    ]
+    for copy in copies:
+        copy.start()
+    pl.semaphore_wait(barrier, SHARDS - 1 + groups - 1)
+    start_sends(me, (0, 1, 2))
+    by_source(EARLY, start_sends)
     for kind in range(3):
         here(kind, me).start()
     by_source(EARLY, start_here)
     by_source(LATE, start_here)
+    for copy in copies:
+        copy.wait()
     constants(c, loads, curve)
-    pl.semaphore_wait(barrier, SHARDS - 1 + groups - 1)
-    start_sends(me, (0, 1, 2))
-    by_source(EARLY, start_sends)
     await_kinds((0, 1, 2), everyone)
-    for kinds, source in GATE:
-        await_kinds(kinds, (source,))
+    tables(c)
     by_source(LATE, start_sends)
-    tables(c)
 
     s_now = jnp.zeros((1, width), F32)
     n_now = jnp.zeros((1, width), F32)
@@ -522,6 +528,17 @@
             device_id={"tm": target}, device_id_type=MESH,
         )
 
+    shifts = sorted(
+        ((dy, dx, dc) for dy in range(groups // 8) for dx in range(4) for dc in range(2)),
+        key=lambda m: -(min(m[0], groups // 8 - m[0]) + min(m[1], 4 - m[1])),
+    )
+    shifts.remove((0, 0, 0))
+
+    def partner(step):
+        dy, dx, dc = shifts[step - 1]
+        y, x, core = lax.div(group, 8), lax.rem(lax.div(group, 2), 4), lax.rem(group, 2)
+        return lax.rem(y + dy, groups // 8) * 8 + lax.rem(x + dx, 4) * 2 + lax.rem(core + dc, 2)
+
     def share(step, source, target):
         return pltpu.make_async_remote_copy(
             src_ref=summed, dst_ref=spread.at[source],
@@ -556,14 +573,14 @@
             line(0, source, source).wait_recv()
 
     for step in range(1, groups):
-        share(step, group, lax.rem(group + step, groups)).start()
+        share(step, group, partner(step)).start()
     for source in everyone:
         values[0:1, source * width : (source + 1) * width] = values_landed[source]
     for step in ORDER:
         block(step, me, lax.rem(me + step, SHARDS)).wait_send()
         line(step, me, lax.rem(me + step, SHARDS)).wait_send()
     for step in range(1, groups):
-        share(step, group, lax.rem(group + step, groups)).wait_send()
+        share(step, group, partner(step)).wait_send()
     for step in range(1, groups):
         source = lax.rem(group + step, groups)
         share(0, source, source).wait_recv()
@@ -594,9 +611,11 @@
             jax.ShapeDtypeStruct((PER, NF), F32),
             jax.ShapeDtypeStruct((1, path_count), F32),
         ],
-        in_specs=[inside] * 2 + [anywhere] * 8,
+        in_specs=[anywhere] * 10,
         out_specs=[inside] * 2,
         scratch_shapes=[
+            pltpu.VMEM((1, NF), F32),
+            pltpu.VMEM((4, NF), F32),
             pltpu.VMEM((SHARDS, PER, 4, width), F32),
             pltpu.VMEM((SHARDS, PER, width), jnp.int32),
             pltpu.VMEM((SHARDS, NF, width), F32),
@@ -626,7 +645,7 @@
         + [dates] * SHARDS
         + [pltpu.VMEM((PER, NF, 128), F32)] * SHARDS
         + [
-            dma((KINDS, SHARDS)), dma((KINDS, SHARDS)), dma((KINDS,)),
+            dma((KINDS, SHARDS)), dma((KINDS, SHARDS)), dma((KINDS + 2,)),
             dma((SHARDS,)), dma((SHARDS,)), dma((SHARDS,)), dma((SHARDS,)),
             dma((groups,)), dma((groups,)),
         ],
@@ -637,7 +656,19 @@
         start_curve.reshape(1, NF), loadings, shocks, exercise_bits, ck_rates, ck_numer,
         ck_survive, vols, regress, date_slot.reshape(1, PER),
     )
+    vega, values = pl.pallas_call(
+        finish_kernel,
+        name="finish",
+        out_shape=[jax.ShapeDtypeStruct(x.shape, F32) for x in (vega, values)],
+        in_specs=[inside] * 2,
+        out_specs=[inside] * 2,
+    )(vega, values)
     return (vega, values.reshape(path_count))
+
+
+def finish_kernel(vega, values, vega_out, values_out):
+    vega_out[...] = vega[...]
+    values_out[...] = values[...]
 
 
 def solution(mesh):

time: 52.8 us -> 51.8 us (0.981)
  local copies, waits for them, and re-layouts: 1.88 us -> 0 us
  Pallas kernels: 50.2 us -> 51 us
    unnamed x4 -> x0, local copies, waits for them, and re-layouts: 1.88 us -> none
    pallas_call x0 -> x1, Pallas kernels: none -> 1.31 us  [local(): pl.pallas_call(finish_kernel, name='finish', out_shape=[jax.ShapeDtypeStr...]
where the time goes in v4:
time: 51.8 us; the launch traced here: 51.7 us
  Pallas kernels  51 us (98%)
  between operations  0.64 us (1%)
    pallas_call x1, Pallas kernels, local(): pl.pallas_call(functools.partial(kernel, NOTIONAL / (path_count * groups)...  49.7 us
    pallas_call x1, Pallas kernels, local(): pl.pallas_call(finish_kernel, name='finish', out_shape=[jax.ShapeDtypeStr...  1.31 us

profile of v4, /device:TPU:1, one launch (start us, length us, event | category | flops | bytes accessed | tf_op | source)
XLA Modules:
  0.0 51.7 jit_solution(6686313144805173825)
XLA Ops:
  0.6 49.7 %pathwise_vega.1 = (f32[5,80]{1,0:T(8,128)}, f32[1,2048]{1,0:T(1,128)}) custom-call(f32[1,80]{1,0:T(1,128)} %bitcast.3, f32[4,80]{1,0:T(4,128)} %loads_in.1, f32[5,4,2048]{2,1,0:T(4,128)} %shocks.1, s32[5,2048]{1,0:T(8,128)} %bits.1, f32[1,80,2048]{2,1,0:T(8,128)} %rates.1, f32[1,2048]{1,0:T(1,128)} %numer.1, f32[1,2048]{1,0:T(1,128)} %survive.1, ...), custom_call_target="tpu_custom_call" | custom-call | tf_op jit(solution)/shard_map/pathwise_vega/pallas_call | solution.py:607
  50.4 1.3 %finish.1 = (f32[5,80]{1,0:T(8,128)}, f32[1,2048]{1,0:T(1,128)}) custom-call(f32[5,80]{1,0:T(8,128)} %get-tuple-element.6.vega, f32[1,2048]{1,0:T(1,128)} %get-tuple-element.7.values), custom_call_target="tpu_custom_call" | custom-call | tf_op jit(solution)/shard_map/finish/pallas_call | solution.py:659
